TPU v7x, 32 devices: a whole 2x2x4 slice. The times are simulated.
32 devices in a mesh: tiles: 16 (over z, y, x), depth: 2 (over core).
Axes of the slice: x: 2, y: 2, z: 4, core: 2. Of those that a mesh axis runs over, the one named last changes fastest.
Arguments:
- momentum: float32 [16, 16, 6300], P('tiles', 'depth'), may hold values from -6 to 6
- tracer: float32 [16, 16, 6300], P('tiles', 'depth'), may hold values from -6 to 6
- mom_diffusivity: float32 [16, 16, 6300], P('tiles', 'depth'), may hold values from 0.02 to 0.2
- tra_diffusivity: float32 [16, 16, 6300], P('tiles', 'depth'), may hold values from 0.02 to 0.2
- mixing: float32 [16, 16, 6300], P('tiles', 'depth'), may hold values from 0.05 to 0.4
- wet_mask: int32 [16, 6300], P('tiles'), may hold values 0 or 1
- neighbours: int32 [16, 4], P('tiles'), may hold values from -1 to 15, as said below
- source_edges: int32 [16, 4], P('tiles'), may hold values from 0 to 3, as said below
- flips: int32 [16, 4], P('tiles'), may hold values from 0 to 1
- mom_cotangent: float32 [16, 16, 6300], P('tiles', 'depth'), may hold values from -6 to 6
- tra_cotangent: float32 [16, 16, 6300], P('tiles', 'depth'), may hold values from -6 to 6
Outputs:
- final_momentum: float32 [16, 16, 6300], P('tiles', 'depth')
- final_tracer: float32 [16, 16, 6300], P('tiles', 'depth')
- grad_momentum: float32 [16, 16, 6300], P('tiles', 'depth')
- grad_tracer: float32 [16, 16, 6300], P('tiles', 'depth')
Inputs may be any that keep to these rules, and one draw needn't show every extreme that they name: `neighbours`: the neighbour relation is symmetric, also across the fold seam, where a tile's north edge faces another tile's north edge in reverse order; -1 marks a missing neighbour. `source_edges`: for north and south directions the facing edge is north or south, for east and west directions it is east or west.
All inputs are finite; a program needn't handle non-finite values. No bound on the sum of `wet_mask` on one device may be relied on, other than what follows from the above.
Results may differ from a plain program's by a relative error of at most 0.00002.
Values sent between devices are 32-bit elements; how exact they have to be, the bound alone decides.
A program may use at most 64 MiB of HBM per device.

v0:
```python
import jax
import jax.numpy as jnp
from jax import lax
from jax.sharding import PartitionSpec as P

NI = 90
NJ = 70


def padded_2(block, sides, width):
    for axis, dim in sides:
        count = lax.axis_size(axis)
        forward = [(i, i + 1) for i in range(count - 1)]
        backward = [(target, source) for source, target in forward]
        low = lax.ppermute(
            lax.slice_in_dim(block, block.shape[dim] - width, None, axis=dim), axis, forward
        )
        high = lax.ppermute(lax.slice_in_dim(block, 0, width, axis=dim), axis, backward)
        block = jnp.concatenate([low, block, high], axis=dim)
    return block


def carried_in(part, axis, combine, identity, reverse):
    count = lax.axis_size(axis)
    place = lax.axis_index(axis)
    ahead = count - 1 - place if reverse else place
    gathered = lax.all_gather(part, axis)
    state = jnp.zeros_like(part) + jnp.asarray(identity, part.dtype)

    def one(hop, state):
        source = count - 1 - hop if reverse else hop
        return combine(state, lax.dynamic_index_in_dim(gathered, source, 0, False))

    return lax.fori_loop(0, ahead, one, state)


def edges_of(field):
    total = field.shape[-1]
    return jnp.concatenate(
        [field[..., total - NI :], field[..., :NI], field[..., NI - 1 :: NI], field[..., ::NI]],
        axis=-1,
    )


def pick_edge(chosen, source, flip, direction):
    if direction < 2:
        strip = jnp.where(source[:, None, None] == 0, chosen[..., :NI], chosen[..., NI : 2 * NI])
    else:
        strip = jnp.where(
            source[:, None, None] == 2,
            chosen[..., 2 * NI : 2 * NI + NJ],
            chosen[..., 2 * NI + NJ :],
        )
    return jnp.where(flip[:, None, None] == 1, strip[..., ::-1], strip)


def select_strips(neighbours, source_edges, flips, carry, pieces):
    spans = [(0, NI), (NI, NI), (2 * NI, NJ), (2 * NI + NJ, NJ)]
    results = []
    for held, piece in zip(carry, pieces):
        count = piece.shape[0]
        strips = []
        for direction in range(4):
            target = neighbours[:, direction]
            valid = (target >= 0) & (target < count)
            row_index = jnp.clip(target, 0, count - 1)
            chosen = jnp.take(piece, row_index, axis=0)
            strip = pick_edge(chosen, source_edges[:, direction], flips[:, direction], direction)
            offset, length = spans[direction]
            strips.append(
                jnp.where(valid[:, None, None], strip, held[..., offset : offset + length])
            )
        results.append(jnp.concatenate(strips, axis=-1))
    return tuple(results)


def shifted_sum(values, halo):
    total = values.shape[-1]
    column = jnp.arange(total) % NI
    north = jnp.concatenate([values[..., NI:], halo[..., :NI]], axis=-1)
    south = jnp.concatenate([halo[..., NI : 2 * NI], values[..., : total - NI]], axis=-1)
    east_halo = jnp.repeat(halo[..., 2 * NI : 2 * NI + NJ], NI, axis=-1)
    west_halo = jnp.repeat(halo[..., 2 * NI + NJ :], NI, axis=-1)
    east = jnp.where(
        column == NI - 1, east_halo, jnp.concatenate([values[..., 1:], values[..., :1]], axis=-1)
    )
    west = jnp.where(
        column == 0, west_halo, jnp.concatenate([values[..., -1:], values[..., :-1]], axis=-1)
    )
    return north + south + east + west


def laplace(field, weighted_halo, wet, wet_halo):
    values = shifted_sum(wet * field, weighted_halo)
    weights = shifted_sum(wet, wet_halo)
    return wet * (values - weights * field)


def add_one(earlier, later):
    return earlier + later


def local(
    momentum,
    tracer,
    mom_diffusivity,
    tra_diffusivity,
    mixing,
    wet_mask,
    neighbours,
    source_edges,
    flips,
    mom_cotangent,
    tra_cotangent,
):
    slot_count = momentum.shape[0]
    level_count = momentum.shape[1]
    edge_cells = 2 * NI + 2 * NJ
    depth_count = lax.axis_size("depth")
    depth_index = lax.axis_index("depth")
    levels_all = level_count * depth_count
    press_scale = levels_all ** (-0.5)
    level_index = depth_index * level_count + jnp.arange(level_count)
    has_above = (level_index > 0).astype(jnp.float32)[None, :, None]
    has_below = (level_index < levels_all - 1).astype(jnp.float32)[None, :, None]

    def fold_strips(carry, pieces):
        return select_strips(neighbours, source_edges, flips, carry, pieces)

    mask_start = jnp.zeros((slot_count, 1, edge_cells), jnp.int32)
    wet_halo = fold_strips(
        (mask_start,),
        (lax.all_gather(edges_of(wet_mask[:, None, :]), "tiles", axis=0, tiled=True),),
    )[0]
    wet_halo = wet_halo.astype(jnp.float32)
    wet = wet_mask[:, None, :].astype(jnp.float32)
    zeros_edge = jnp.zeros((slot_count, level_count, edge_cells), jnp.float32)
    zeros_cells = jnp.zeros((slot_count, momentum.shape[2]), jnp.float32)

    def vertical_from(field, above, below):
        return has_above * (above - field) + has_below * (below - field)

    def level_halo(field):
        padded = padded_2(field, (("depth", 1),), 1)
        return (padded[:, :-2], padded[:, 2:])

    mom_now, tra_now = (momentum, tracer)
    for iteration in range(2):
        own_sum = jnp.cumsum(tra_now, axis=1)
        above, below = level_halo(tra_now)
        prior_own = carried_in(own_sum[:, -1], "depth", add_one, zeros_cells, False)
        press = press_scale * (own_sum + prior_own[:, None, :])
        mom_halo, tra_halo, press_halo = fold_strips(
            (zeros_edge, zeros_edge, zeros_edge),
            (
                lax.all_gather(edges_of(mom_now), "tiles", axis=0, tiled=True),
                lax.all_gather(edges_of(tra_now), "tiles", axis=0, tiled=True),
                lax.all_gather(edges_of(press), "tiles", axis=0, tiled=True),
            ),
        )
        mom_next = (
            mom_now
            + mom_diffusivity * laplace(mom_now, wet_halo * mom_halo, wet, wet_halo)
            - 0.1 * laplace(press, wet_halo * press_halo, wet, wet_halo)
        )
        tra_next = (
            tra_now
            + tra_diffusivity * laplace(tra_now, wet_halo * tra_halo, wet, wet_halo)
            + mixing * vertical_from(tra_now, above, below)
            + 0.2 * mom_now
        )
        mom_now, tra_now = (mom_next, tra_next)
    mom_adjoint, tra_adjoint = (mom_cotangent, tra_cotangent)
    for iteration in range(2):
        mom_weighted = mom_diffusivity * mom_adjoint
        tra_weighted = tra_diffusivity * tra_adjoint
        cycle_mom, cycle_plain, cycle_tra = fold_strips(
            (zeros_edge, zeros_edge, zeros_edge),
            (
                lax.all_gather(edges_of(wet * mom_weighted), "tiles", axis=0, tiled=True),
                lax.all_gather(edges_of(wet * mom_adjoint), "tiles", axis=0, tiled=True),
                lax.all_gather(edges_of(wet * tra_weighted), "tiles", axis=0, tiled=True),
            ),
        )
        press_adjoint = -0.1 * laplace(mom_adjoint, cycle_plain, wet, wet_halo)
        mixed = mixing * tra_adjoint
        later_sum = jnp.flip(jnp.cumsum(jnp.flip(press_adjoint, axis=1), axis=1), axis=1)
        after = carried_in(later_sum[:, 0], "depth", add_one, zeros_cells, True)
        above, below = level_halo(mixed)
        press_back = press_scale * (later_sum + after[:, None, :])
        mom_back = mom_adjoint + laplace(mom_weighted, cycle_mom, wet, wet_halo) + 0.2 * tra_adjoint
        tra_back = (
            tra_adjoint
            + laplace(tra_weighted, cycle_tra, wet, wet_halo)
            + vertical_from(mixed, above, below)
            + press_back
        )
        mom_adjoint, tra_adjoint = (mom_back, tra_back)
    return (mom_now, tra_now, mom_adjoint, tra_adjoint)


def solution(mesh):
    in_specs = (
        P("tiles", "depth", None),
        P("tiles", "depth", None),
        P("tiles", "depth", None),
        P("tiles", "depth", None),
        P("tiles", "depth", None),
        P("tiles", None),
        P("tiles", None),
        P("tiles", None),
        P("tiles", None),
        P("tiles", "depth", None),
        P("tiles", "depth", None),
    )
    out_specs = (
        P("tiles", "depth", None),
        P("tiles", "depth", None),
        P("tiles", "depth", None),
        P("tiles", "depth", None),
    )
    return jax.shard_map(local, mesh=mesh, in_specs=in_specs, out_specs=out_specs, check_vma=False)
```

profile of v0, /device:TPU:0, one launch (start us, length us, event | category | flops | bytes accessed | tf_op | source)
XLA Modules:
  0.0 668.3 jit_solution(13493256316628074655)
XLA Ops:
  1.5 1.1 broadcast_multiply_fusion.6
  19.5 42.5 %all_gather.51 = s32[16,1,320]{2,1,0:T(1,128)S(1)} all-gather(s32[1,1,320]{2,1,0:T(1,128)S(1)} %pad_add_fusion), channel_id=1, replica_groups=mesh['tiles'=16,'depth'=2] {'tiles'}, dimensions={0}, use_global_device_ids=true | all-gather | bytes 21760 | tf_op jit(solution)/shard_map/all_gather | solution.py:133
  65.6 36.5 %all_gather.60 = f32[16,8,320]{2,1,0:T(8,128)S(1)} all-gather(f32[1,8,320]{2,1,0:T(8,128)S(1)} %pad_maximum_fusion.14), channel_id=1, replica_groups=mesh['tiles'=16,'depth'=2] {'tiles'}, dimensions={0}, use_global_device_ids=true | all-gather | bytes 174080 | tf_op jit(solution)/shard_map/all_gather | solution.py:180
  103.1 38.7 %all_gather.56 = f32[16,8,320]{2,1,0:T(8,128)S(1)} all-gather(f32[1,8,320]{2,1,0:T(8,128)S(1)} %pad_maximum_fusion.11), channel_id=1, replica_groups=mesh['tiles'=16,'depth'=2] {'tiles'}, dimensions={0}, use_global_device_ids=true | all-gather | bytes 174080 | tf_op jit(solution)/shard_map/all_gather | solution.py:157
  144.7 2.0 broadcast_multiply_fusion.12
  146.7 1.0 broadcast_multiply_fusion.8
  148.3 1.9 collective-permute-start.4
  150.2 1.3 collective-permute-start.5
  152.2 4.2 collective-permute-start
  156.4 1.3 collective-permute-start.1
  167.8 36.6 %all_gather.66 = f32[16,8,320]{2,1,0:T(8,128)S(1)} all-gather(f32[1,8,320]{2,1,0:T(8,128)S(1)} %pad_maximum_fusion.19), channel_id=1, replica_groups=mesh['tiles'=16,'depth'=2] {'tiles'}, dimensions={0}, use_global_device_ids=true | all-gather | bytes 174080 | tf_op jit(solution)/shard_map/all_gather | solution.py:181
  207.8 1.3 fusion.95
  212.8 38.4 %all_gather.52 = f32[16,8,320]{2,1,0:T(8,128)S(1)} all-gather(f32[1,8,320]{2,1,0:T(8,128)S(1)} %pad_maximum_fusion.8), channel_id=1, replica_groups=mesh['tiles'=16,'depth'=2] {'tiles'}, dimensions={0}, use_global_device_ids=true | all-gather | bytes 174080 | tf_op jit(solution)/shard_map/all_gather | solution.py:156
  259.5 36.6 %all_gather.62 = f32[16,8,320]{2,1,0:T(8,128)S(1)} all-gather(f32[1,8,320]{2,1,0:T(8,128)S(1)} %pad_maximum_fusion.16), channel_id=1, replica_groups=mesh['tiles'=16,'depth'=2] {'tiles'}, dimensions={0}, use_global_device_ids=true | all-gather | bytes 174080 | tf_op jit(solution)/shard_map/all_gather | solution.py:182
  297.8 38.4 %all_gather.63 = f32[16,8,320]{2,1,0:T(8,128)S(1)} all-gather(f32[1,8,320]{2,1,0:T(8,128)S(1)} %pad_maximum_fusion.17), channel_id=1, replica_groups=mesh['tiles'=16,'depth'=2] {'tiles'}, dimensions={0}, use_global_device_ids=true | all-gather | bytes 174080 | tf_op jit(solution)/shard_map/all_gather | solution.py:181
  339.7 1.5 fusion.86
  342.2 1.8 all_gather.64
  345.0 36.6 %all_gather.61 = f32[16,8,320]{2,1,0:T(8,128)S(1)} all-gather(f32[1,8,320]{2,1,0:T(8,128)S(1)} %pad_maximum_fusion.15), channel_id=1, replica_groups=mesh['tiles'=16,'depth'=2] {'tiles'}, dimensions={0}, use_global_device_ids=true | all-gather | bytes 174080 | tf_op jit(solution)/shard_map/all_gather | solution.py:180
  383.4 1.8 all_gather.67
  385.6 1.8 all_gather.53
  389.1 14.9 %rev.214 = f32[1,8,6300]{2,1,0:T(8,128)} reverse(f32[1,8,6300]{2,1,0:T(8,128)S(1)} %reduce_window_sum.27), dimensions={1} | reverse | bytes 403200 | tf_op jit(solution)/shard_map/jit(_flip)/rev | solution.py:187
  406.7 0.8 broadcast_in_dim.958
  407.7 0.8 broadcast_in_dim.960
  412.6 1.7 broadcast_multiply_fusion.2
  416.5 1.0 fusion.165
  421.3 1.5 broadcast_multiply_fusion.7
  423.3 1.8 all_gather.57
  426.8 1.1 slice.1238
  427.9 1.1 slice.1239
  429.4 38.4 %all_gather.59 = f32[16,8,320]{2,1,0:T(8,128)S(1)} all-gather(f32[1,8,320]{2,1,0:T(8,128)S(1)} %pad_maximum_fusion.13), channel_id=1, replica_groups=mesh['tiles'=16,'depth'=2] {'tiles'}, dimensions={0}, use_global_device_ids=true | all-gather | bytes 174080 | tf_op jit(solution)/shard_map/all_gather | solution.py:157
  468.8 36.7 %all_gather.54 = f32[16,8,320]{2,1,0:T(8,128)S(1)} all-gather(f32[1,8,320]{2,1,0:T(8,128)S(1)} %pad_maximum_fusion.9), channel_id=1, replica_groups=mesh['tiles'=16,'depth'=2] {'tiles'}, dimensions={0}, use_global_device_ids=true | all-gather | bytes 174080 | tf_op jit(solution)/shard_map/all_gather | solution.py:158
  506.5 38.4 %all_gather.58 = f32[16,8,320]{2,1,0:T(8,128)S(1)} all-gather(f32[1,8,320]{2,1,0:T(8,128)S(1)} %pad_maximum_fusion.12), channel_id=1, replica_groups=mesh['tiles'=16,'depth'=2] {'tiles'}, dimensions={0}, use_global_device_ids=true | all-gather | bytes 174080 | tf_op jit(solution)/shard_map/all_gather | solution.py:158
  551.8 0.8 fusion.201
  556.4 36.8 %all_gather.65 = f32[16,8,320]{2,1,0:T(8,128)S(1)} all-gather(f32[1,8,320]{2,1,0:T(8,128)S(1)} %pad_maximum_fusion.18), channel_id=1, replica_groups=mesh['tiles'=16,'depth'=2] {'tiles'}, dimensions={0}, use_global_device_ids=true | all-gather | bytes 174080 | tf_op jit(solution)/shard_map/all_gather | solution.py:182
  595.2 1.9 collective-permute-start.2
  597.1 1.3 collective-permute-start.3
  599.2 0.8 broadcast_in_dim.972
  601.0 4.2 collective-permute-start.6
  605.2 1.3 collective-permute-start.7
  606.6 0.8 broadcast_in_dim.924
  607.6 0.8 broadcast_in_dim.927
  608.5 0.8 broadcast_in_dim.934
  612.4 0.8 broadcast_in_dim.946
  613.4 0.8 broadcast_in_dim.948
  615.0 3.4 fusion.19
  619.9 38.2 %all_gather.55 = f32[16,8,320]{2,1,0:T(8,128)S(1)} all-gather(f32[1,8,320]{2,1,0:T(8,128)S(1)} %pad_maximum_fusion.10), channel_id=1, replica_groups=mesh['tiles'=16,'depth'=2] {'tiles'}, dimensions={0}, use_global_device_ids=true | all-gather | bytes 174080 | tf_op jit(solution)/shard_map/all_gather | solution.py:156
  663.1 2.7 fusion.48
  666.5 1.7 fusion.4
  (553 shorter events, 92.7 us)
Async XLA Ops:
  1.4 7.8 %copy-start.3 = (f32[1,8,6300]{2,1,0:T(8,128)S(1)}, f32[1,8,6300]{2,1,0:T(8,128)}, u32[]{:S(2)}) copy-start(f32[1,8,6300]{2,1,0:T(8,128)} %param.24) | copy-start | bytes 604804
  6.6 5.6 copy-start.23
  102.7 43.9 %copy-start.6 = (f32[1,8,6300]{2,1,0:T(8,128)S(1)}, f32[1,8,6300]{2,1,0:T(8,128)}, u32[]{:S(2)}) copy-start(f32[1,8,6300]{2,1,0:T(8,128)} %param.33) | copy-start | bytes 604804
  103.1 43.5 %copy-start.5 = (f32[1,8,6300]{2,1,0:T(8,128)S(1)}, f32[1,8,6300]{2,1,0:T(8,128)}, u32[]{:S(2)}) copy-start(f32[1,8,6300]{2,1,0:T(8,128)} %param.32) | copy-start | bytes 604804
  142.4 4.2 copy-start.2
  143.1 3.6 copy-start.1
  143.2 3.5 copy-start
  148.3 263.5 %collective-permute-start.4 = (f32[1,1,6300]{2,1,0:T(1,128)}, f32[1,1,6300]{2,1,0:T(1,128)}, u32[]{:S(2)}, u32[]{:S(2)}) collective-permute-start(f32[1,1,6300]{2,1,0:T(1,128)} %get-tuple-element.272), channel_id=1, source_target_pairs={{0,1},{2,3},{4,5},{6,7},{8,9},{10,11},{12,13},{14,15},{16,17},{18,... | collective-permute-start | bytes 75608 | tf_op jit(solution)/shard_map/ppermute | solution.py:15
  150.2 261.7 %collective-permute-start.5 = (f32[1,1,6300]{2,1,0:T(1,128)}, f32[1,1,6300]{2,1,0:T(1,128)}, u32[]{:S(2)}, u32[]{:S(2)}) collective-permute-start(f32[1,1,6300]{2,1,0:T(1,128)} %get-tuple-element.273), channel_id=1, source_target_pairs={{1,0},{3,2},{5,4},{7,6},{9,8},{11,10},{13,12},{15,14},{17,16},{19,... | collective-permute-start | bytes 75608 | tf_op jit(solution)/shard_map/ppermute | solution.py:18
  152.2 268.4 %collective-permute-start = (f32[1,1,6300]{2,1,0:T(1,128)}, f32[1,1,6300]{2,1,0:T(1,128)}, u32[]{:S(2)}, u32[]{:S(2)}) collective-permute-start(f32[1,1,6300]{2,1,0:T(1,128)} %get-tuple-element.349), channel_id=1, source_target_pairs={{0,1},{2,3},{4,5},{6,7},{8,9},{10,11},{12,13},{14,15},{16,17},{18,... | collective-permute-start | bytes 75608 | tf_op jit(solution)/shard_map/ppermute | solution.py:15
  156.4 264.2 %collective-permute-start.1 = (f32[1,1,6300]{2,1,0:T(1,128)}, f32[1,1,6300]{2,1,0:T(1,128)}, u32[]{:S(2)}, u32[]{:S(2)}) collective-permute-start(f32[1,1,6300]{2,1,0:T(1,128)} %get-tuple-element.350), channel_id=1, source_target_pairs={{1,0},{3,2},{5,4},{7,6},{9,8},{11,10},{13,12},{15,14},{17,16},{19,... | collective-permute-start | bytes 75608 | tf_op jit(solution)/shard_map/ppermute | solution.py:18
  205.3 1.9 copy-start.4
  251.2 3.1 copy-start.95
  296.9 0.7 copy-start.66
  296.9 0.7 copy-start.73
  296.9 0.8 copy-start.74
  337.7 1.3 copy-start.12
  389.1 22.8 %copy-start.77 = (f32[8]{0:T(128)}, f32[8]{0:T(128)S(1)}, u32[]{:S(2)}) copy-start(f32[8]{0:T(128)S(1)} %get-tuple-element.455) | copy-start | bytes 100
  389.1 22.8 %copy-start.81 = (f32[8]{0:T(128)}, f32[8]{0:T(128)S(1)}, u32[]{:S(2)}) copy-start(f32[8]{0:T(128)S(1)} %get-tuple-element.456) | copy-start | bytes 100
  415.0 1.5 copy-start.10
  415.0 1.5 copy-start.11
  415.0 1.5 copy-start.16
  415.0 1.5 copy-start.17
  417.6 3.0 copy-start.9
  425.2 0.7 copy-start.22
  425.2 0.8 copy-start.19
  595.2 19.0 %collective-permute-start.2 = (f32[1,1,6300]{2,1,0:T(1,128)}, f32[1,1,6300]{2,1,0:T(1,128)}, u32[]{:S(2)}, u32[]{:S(2)}) collective-permute-start(f32[1,1,6300]{2,1,0:T(1,128)} %get-tuple-element.339), channel_id=1, source_target_pairs={{0,1},{2,3},{4,5},{6,7},{8,9},{10,11},{12,13},{14,15},{16,17},{18,... | collective-permute-start | bytes 75608 | tf_op jit(solution)/shard_map/ppermute | solution.py:15
  597.1 17.2 %collective-permute-start.3 = (f32[1,1,6300]{2,1,0:T(1,128)}, f32[1,1,6300]{2,1,0:T(1,128)}, u32[]{:S(2)}, u32[]{:S(2)}) collective-permute-start(f32[1,1,6300]{2,1,0:T(1,128)} %get-tuple-element.340), channel_id=1, source_target_pairs={{1,0},{3,2},{5,4},{7,6},{9,8},{11,10},{13,12},{15,14},{17,16},{19,... | collective-permute-start | bytes 75608 | tf_op jit(solution)/shard_map/ppermute | solution.py:18
  601.0 64.8 %collective-permute-start.6 = (f32[1,1,6300]{2,1,0:T(1,128)}, f32[1,1,6300]{2,1,0:T(1,128)}, u32[]{:S(2)}, u32[]{:S(2)}) collective-permute-start(f32[1,1,6300]{2,1,0:T(1,128)} %get-tuple-element.260), channel_id=1, source_target_pairs={{0,1},{2,3},{4,5},{6,7},{8,9},{10,11},{12,13},{14,15},{16,17},{18,... | collective-permute-start | bytes 75608 | tf_op jit(solution)/shard_map/ppermute | solution.py:15
  605.2 60.6 %collective-permute-start.7 = (f32[1,1,6300]{2,1,0:T(1,128)}, f32[1,1,6300]{2,1,0:T(1,128)}, u32[]{:S(2)}, u32[]{:S(2)}) collective-permute-start(f32[1,1,6300]{2,1,0:T(1,128)} %get-tuple-element.261), channel_id=1, source_target_pairs={{1,0},{3,2},{5,4},{7,6},{9,8},{11,10},{13,12},{15,14},{17,16},{19,... | collective-permute-start | bytes 75608 | tf_op jit(solution)/shard_map/ppermute | solution.py:18
  613.4 0.9 copy-start.13
  613.4 0.9 copy-start.45
  613.4 0.9 copy-start.46
  613.4 0.9 copy-start.47
  614.2 0.8 copy-start.18
  614.2 0.8 copy-start.44
  614.3 0.7 copy-start.29
  614.3 0.7 copy-start.28
  614.3 0.7 copy-start.79
  614.3 0.7 copy-start.83
  661.5 0.9 copy-start.42
  663.1 2.8 copy-start.7
  663.1 2.8 copy-start.8
  663.1 2.8 copy-start.14
  663.1 2.8 copy-start.15
  663.1 2.8 copy-start.21
  663.1 2.8 copy-start.36
  663.1 2.8 copy-start.43
  (56 other events, 37.5 us)
where the time goes:
time: 670 us; the launch traced here: 668 us
  blocking collectives  500 us (75%)
  local copies, waits for them, and re-layouts  98.7 us (15%)
  other arithmetic  37 us (6%)
  starting transfers between devices  17.3 us (3%)
  between operations  15 us (2%)
    all_gather x2, blocking collectives, local(): lax.all_gather(edges_of(tra_now), 'tiles', axis=0, tiled=True)  77.1 us
    all_gather x2, blocking collectives, local(): lax.all_gather(edges_of(mom_now), 'tiles', axis=0, tiled=True)  76.6 us
    all_gather x2, blocking collectives, local(): lax.all_gather(edges_of(press), 'tiles', axis=0, tiled=True)  75 us
    all_gather x2, blocking collectives, local(): lax.all_gather(edges_of(wet * mom_adjoint), 'tiles', axis=0, tiled=True)  75 us
    all_gather x2, blocking collectives, local(): lax.all_gather(edges_of(wet * tra_weighted), 'tiles', axis=0, tiled=True)  73.4 us
    all_gather x2, blocking collectives, local(): lax.all_gather(edges_of(wet * mom_weighted), 'tiles', axis=0, tiled=True)  73.1 us
    all_gather x1, blocking collectives, local(): lax.all_gather(edges_of(wet_mask[:, None, :]), 'tiles', axis=0, tiled=True)  42.5 us
    rev x2, local copies, waits for them, and re-layouts, local(): jnp.flip(jnp.cumsum(jnp.flip(press_adjoint, axis=1), axis=1), axis=1)  15.6 us
  transfers between devices with their start and end apart: 8, of which 0 were waited for; matrix products, arithmetic and copies ran while one was open for 13% of the time, Pallas kernels for 0%

commit v1 on v0

v1 whole, which is shorter than its diff:
```python
import functools

import jax
import jax.numpy as jnp
from jax import lax
from jax.experimental import pallas as pl
from jax.experimental.pallas import tpu as pltpu
from jax.sharding import PartitionSpec as P

NI = 90
NJ = 70
CELLS = NI * NJ
LANES = 128
LO = LANES
HI = LANES + CELLS
WIDTH = -(-(HI + NI) // LANES) * LANES
CHUNKS = WIDTH // LANES
FIRST = 64 * NI // LANES
MESH = pl.DeviceIdType.MESH
EXACT = lax.Precision.HIGHEST


def roll(x, shift, axis=1):
    return pltpu.roll(x, shift % x.shape[axis], axis)


def kernel(
    inner, outer, depth, levels_all,
    mom_ref, tra_ref, mdif_ref, tdif_ref, mix_ref, wet_ref, nb_ref, se_ref, fl_ref, mcot_ref, tcot_ref,
    mom_out, tra_out, mgrad_out, tgrad_out,
    table, tables, tables_s, grid, gath_0, gath_1, part, halo, edge_s, edge_r, carry_s, carry_r,
    tab_send, tab_recv, tab_local, g_send, g_recv, h_send, h_recv, e_send, e_recv, c_send, c_recv,
):
    me = lax.axis_index("tiles")
    d = lax.axis_index("depth")
    member = lax.rem(me, inner)
    group = lax.div(me, inner)
    rows = mom_ref.shape[1]
    total = grid.shape[0]
    press = -0.1 * levels_all ** (-0.5)

    def in_inner(o):
        return {"tiles": group * inner + lax.rem(member + o, inner), "depth": d}

    def in_outer(o):
        return {"tiles": lax.rem(group + o, outer) * inner + member, "depth": d}

    def in_depth(o):
        return {"tiles": me, "depth": lax.rem(d + o, depth)}

    barrier = pltpu.get_barrier_semaphore()
    for count, where_to in ((inner, in_inner), (outer, in_outer), (depth, in_depth)):
        for o in range(1, count):
            pl.semaphore_signal(barrier, inc=1, device_id=where_to(o), device_id_type=MESH)
    pl.semaphore_wait(barrier, inner + outer + depth - 3)

    started = []

    def send(src, dst, ssem, rsem, to):
        copy = pltpu.make_async_remote_copy(
            src_ref=src, dst_ref=dst, send_sem=ssem, recv_sem=rsem, device_id=to, device_id_type=MESH
        )
        copy.start()
        started.append(copy)
        return copy

    table[...] = jnp.zeros_like(table)
    table[0:1, 0:4] = nb_ref[...]
    table[1:2, 0:4] = se_ref[...]
    table[2:3, 0:4] = fl_ref[...]
    tables[group] = table[...]
    table_copies = [
        send(table, tables.at[group], tab_send.at[o], tab_recv.at[o], in_outer(o)) for o in range(1, outer)
    ]

    pos = (lax.broadcasted_iota(jnp.int32, (8, WIDTH), 1) - LO).astype(jnp.float32)
    col = pos - NI * jnp.floor((pos + 0.5) * (1.0 / NI))
    inside = (pos > -0.5) & (pos < CELLS - 0.5)
    at_west = (col < 0.5) & inside
    at_east = (col > NI - 1.5) & inside
    on_edge = jnp.where(at_west | at_east, 1.0, 0.0)
    lane = lax.broadcasted_iota(jnp.int32, (total, LANES), 1)
    odd = lax.rem(lane, 2) == 1
    level = lax.broadcasted_iota(jnp.int32, (rows, CELLS), 0)

    r0 = lax.broadcasted_iota(jnp.int32, (LANES, LANES), 0)
    r1 = lax.broadcasted_iota(jnp.int32, (LANES, LANES), 1)
    rev_i = jnp.where(r0 + r1 == NI - 1, 1.0, 0.0)

    wet = jnp.broadcast_to(wet_ref[...].astype(jnp.float32), (rows, CELLS))
    mdif, tdif, mix = mdif_ref[0], tdif_ref[0], mix_ref[0]

    def running(x, down):
        k = 1
        while k < rows:
            if down:
                x = x + jnp.where(level >= k, roll(x, k, 0), 0.0)
            else:
                x = x + jnp.where(level < rows - k, roll(x, rows - k, 0), 0.0)
            k *= 2
        return x

    grid[...] = jnp.zeros_like(grid)
    m, s, lm, lt = mom_ref[0], tra_ref[0], mcot_ref[0], tcot_ref[0]
    has_above = jnp.where(d > 0, 1.0, 0.0)
    has_below = jnp.where(d < depth - 1, 1.0, 0.0)
    weights = None

    for r in range(2):
        gath = (gath_0, gath_1)[r]
        mixed = mix * lt
        edge_copies = []
        if depth > 1:
            edge_s[r, 0, 0:1] = s[rows - 1 : rows]
            edge_s[r, 0, 1:2] = mixed[rows - 1 : rows]
            edge_s[r, 1, 0:1] = s[0:1]
            edge_s[r, 1, 1:2] = mixed[0:1]
            for i, o in ((0, 1), (1, depth - 1)):
                edge_copies.append(
                    send(edge_s.at[r, i], edge_r.at[r, i], e_send.at[r, i], e_recv.at[r, i], in_depth(o))
                )
        back = running(lm, False)
        u = tdif * lt + press * back
        w_m = mdif * lm
        t_sum = press * back[0:1]
        grid[0:rows, LO:HI] = wet * m
        grid[rows : 2 * rows, LO:HI] = wet * s
        grid[2 * rows : 3 * rows, LO:HI] = wet * w_m
        grid[3 * rows : 4 * rows, LO:HI] = wet * u
        grid[4 * rows : 5 * rows, LO:HI] = jnp.where(level == 0, wet, jnp.where(level == 1, wet * t_sum, 0.0))

        gath[member, 0] = roll(grid[:, WIDTH - 2 * LANES : WIDTH], -(HI - NI - (WIDTH - 2 * LANES)))[:, :LANES]
        gath[member, 1] = grid[:, LO : LO + LANES]
        for g in range(5):
            span = slice(g * rows, (g + 1) * rows)
            for part_of, (a, b) in enumerate(((1, 1 + FIRST), (1 + FIRST, CHUNKS))):
                acc = None
                for v in range(a, b):
                    cut = slice(v * LANES, (v + 1) * LANES)
                    piece = grid[span, cut] * on_edge[:, cut]
                    acc = piece if acc is None else acc + piece
                gath[member, 2 + part_of, span] = acc
        copies = [
            send(gath.at[member], gath.at[member], g_send.at[r, o], g_recv.at[r, o], in_inner(o))
            for o in range(1, inner)
        ]
        if r == 0:
            for copy in table_copies:
                copy.wait_recv()
            local = pltpu.make_async_copy(tables, tables_s, tab_local)
            local.start()
            local.wait()
        for copy in copies:
            copy.wait_recv()

        def strips_for(target):
            def source(direction):
                tile = tables_s[target, 0, direction]
                edge = tables_s[target, 1, direction]
                known = jnp.maximum(tile, 0)
                here = (tile >= 0) & (lax.div(known, inner) == group)
                return lax.rem(known, inner), edge, jnp.where(here, 1.0, 0.0)

            result = []
            for direction in range(2):
                tile, edge, here = source(direction)
                result.append(gath[tile, jnp.where(edge == 0, 0, 1)] * here)
            east, east_edge, east_here = source(2)
            west, west_edge, west_here = source(3)
            east_turn = jnp.where(east_edge == 3, 1.0, 0.0)
            west_turn = jnp.where(west_edge == 2, 1.0, 0.0)
            for k in (2, 3):
                e = gath[east, k]
                e = (roll(e, NI - 1) * east_turn + e * (1.0 - east_turn)) * east_here
                w = gath[west, k]
                w = (roll(w, 1 - NI) * west_turn + w * (1.0 - west_turn)) * west_here
                result.append(jnp.where(odd, e, w))
            return result

        copies = []
        for o in range(1, outer):
            for k, strip in enumerate(strips_for(lax.rem(group + o, outer))):
                part[r, o, k] = strip
            copies.append(send(part.at[r, o], halo.at[r, o], h_send.at[r, o], h_recv.at[r, o], in_outer(o)))
        strips = strips_for(group)
        for o in range(1, outer):
            copies[o - 1].wait_recv()
            for k in range(4):
                strips[k] = strips[k] + halo[r, o, k]

        flip = [jnp.where(tables_s[group, 2, k] == 1, 1.0, 0.0) for k in range(4)]
        dot = functools.partial(jnp.dot, precision=EXACT, preferred_element_type=jnp.float32)
        north = dot(strips[0], rev_i) * flip[0] + strips[0] * (1.0 - flip[0])
        south = dot(strips[1], rev_i) * flip[1] + strips[1] * (1.0 - flip[1])
        both = lax.rem(r0, 2) == 0
        aim = jnp.where(both, NI * (NJ - 1) % LANES, (NI * (NJ - 1) + 2 * (NI - 1)) % LANES)
        turn = jnp.where(lax.rem(r0 + r1 + LANES * 4 - aim, LANES) == 0, 1.0, 0.0)
        one, two = dot(strips[2], turn), dot(strips[3], turn)
        tail = jnp.zeros((total, LANES), jnp.float32)
        for j in range(NJ - 64):
            for x in (NI * j % LANES, (NI * j + NI - 1) % LANES):
                tail = jnp.where(lane == x, 1.0, tail)
        turned_one = jnp.where(tail > 0.5, two, one)
        turned_two = jnp.where(tail > 0.5, one, 0.0)
        ew_flip = jnp.where(odd, flip[2], flip[3])
        ew_one = jnp.where(ew_flip > 0.5, turned_one, strips[2])
        ew_two = jnp.where(ew_flip > 0.5, turned_two, strips[3])

        grid[:, 0:LANES] = roll(south, LANES - NI)
        end = WIDTH - LANES
        grid[:, end:] = jnp.where(lane < HI - end, grid[:, end:], roll(north, HI - end))

        def around(g):
            span = slice(g * rows, (g + 1) * rows)
            x = grid[span, :]
            side = jnp.concatenate(
                [ew_one[span]] * (1 + FIRST) + [ew_two[span]] * (CHUNKS - 1 - FIRST), axis=1
            )
            east = jnp.where(at_east, side, roll(x, -1))
            west = jnp.where(at_west, side, roll(x, 1))
            return (roll(x, -NI) + roll(x, NI) + east + west)[:, LO:HI]

        extra = around(4)
        weights = extra[0:1]
        lap_t = wet[0:1] * (extra[1:2] - weights * t_sum)
        lap_s = wet * (around(1) - weights * s)
        sums = running(lap_s, True)
        copies = []
        if depth > 1:
            carry_s[r, 0:1] = sums[rows - 1 : rows]
            carry_s[r, 1:2] = lap_t
            copies = [
                send(carry_s.at[r], carry_r.at[r, o], c_send.at[r, o], c_recv.at[r, o], in_depth(o))
                for o in range(1, depth)
            ]
        lap_m = wet * (around(0) - weights * m)
        lap_w = wet * (around(2) - weights * w_m)
        lap_u = wet * (around(3) - weights * u)
        m_next = m + mdif * lap_m + press * sums
        lm_next = lm + lap_w + 0.2 * lt

        for copy in edge_copies:
            copy.wait_recv()

        def vertical(q, which):
            above, below = q[0:1], q[rows - 1 : rows]
            if depth > 1:
                above = edge_r[r, 0, which : which + 1] * has_above + above * (1.0 - has_above)
                below = edge_r[r, 1, which : which + 1] * has_below + below * (1.0 - has_below)
            up = jnp.where(level == 0, above, roll(q, 1, 0))
            down = jnp.where(level == rows - 1, below, roll(q, rows - 1, 0))
            return (up - q) + (down - q)

        s_next = s + tdif * lap_s + mix * vertical(s, 0) + 0.2 * m
        lt_next = lt + lap_u + vertical(mixed, 1)
        for o in range(1, depth):
            copies[o - 1].wait_recv()
            origin = lax.rem(d + depth - o, depth)
            m_next = m_next + carry_r[r, o, 0:1] * jnp.where(origin < d, press, 0.0)
            lt_next = lt_next + carry_r[r, o, 1:2] * jnp.where(origin > d, 1.0, 0.0)
        m, s, lm, lt = m_next, s_next, lm_next, lt_next

    mom_out[0] = m
    tra_out[0] = s
    mgrad_out[0] = lm
    tgrad_out[0] = lt
    for copy in started:
        copy.wait_send()


def solution(mesh):
    tiles, depth = mesh.shape["tiles"], mesh.shape["depth"]
    inner = max(k for k in range(1, tiles + 1) if tiles % k == 0 and k * k <= tiles)
    outer = tiles // inner

    def local(*args):
        rows = args[0].shape[1]
        total = 5 * rows
        dma = pltpu.SemaphoreType.DMA
        f32 = jnp.float32
        shape = jax.ShapeDtypeStruct(args[0].shape, f32)
        vmem = pl.BlockSpec(memory_space=pltpu.VMEM)
        return pl.pallas_call(
            functools.partial(kernel, inner, outer, depth, rows * depth),
            out_shape=(shape,) * 4,
            in_specs=[vmem] * 11,
            out_specs=(vmem,) * 4,
            scratch_shapes=[
                pltpu.VMEM((8, LANES), jnp.int32),
                pltpu.VMEM((outer, 8, LANES), jnp.int32),
                pltpu.SMEM((outer, 8, LANES), jnp.int32),
                pltpu.VMEM((total, WIDTH), f32),
                pltpu.VMEM((inner, 4, total, LANES), f32),
                pltpu.VMEM((inner, 4, total, LANES), f32),
                pltpu.VMEM((2, outer, 4, total, LANES), f32),
                pltpu.VMEM((2, outer, 4, total, LANES), f32),
                pltpu.VMEM((2, 2, 2, CELLS), f32),
                pltpu.VMEM((2, 2, 2, CELLS), f32),
                pltpu.VMEM((2, 2, CELLS), f32),
                pltpu.VMEM((2, depth, 2, CELLS), f32),
                dma((outer,)), dma((outer,)), dma(()),
                dma((2, inner)), dma((2, inner)),
                dma((2, outer)), dma((2, outer)),
                dma((2, 2)), dma((2, 2)),
                dma((2, depth)), dma((2, depth)),
            ],
            compiler_params=pltpu.CompilerParams(
                collective_id=0, has_side_effects=True, vmem_limit_bytes=48 * 1024 * 1024
            ),
        )(*args)

    whole = P("tiles", "depth", None)
    flat = P("tiles", None)
    in_specs = (whole,) * 5 + (flat,) * 4 + (whole,) * 2
    return jax.shard_map(local, mesh=mesh, in_specs=in_specs, out_specs=(whole,) * 4, check_vma=False)
```

time: 670 us -> 50 us (0.07)
  blocking collectives: 500 us -> 0 us
  local copies, waits for them, and re-layouts: 98.7 us -> 11.9 us
  Pallas kernels: 0 us -> 37.1 us
  other arithmetic: 37 us -> 0 us
  starting transfers between devices: 17.3 us -> 0 us
  between operations: 15 us -> 0.66 us
    all_gather x17 -> x0, blocking collectives: 500 us -> none  [the longest x2 77.1 us: local(): lax.all_gather(edges_of(tra_now), 'tiles', axis=0, tiled=True)]
    slice x102 -> x0, local copies, waits for them, and re-layouts: 44 us -> none  [the longest x8 5.87 us: shifted_sum(): values[..., :total - NI]]
    pallas_call x0 -> x1, Pallas kernels: none -> 37.1 us  [local(): pl.pallas_call(functools.partial(kernel, inner, outer, depth, rows * dept...]
    broadcast_in_dim x56 -> x0, local copies, waits for them, and re-layouts: 21.4 us -> none  [the longest x26 11 us: shifted_sum(): east_halo = jnp.repeat(halo[..., 2 * NI:2 * NI + NJ], NI, axis=-1)]
    rev x54 -> x0, local copies, waits for them, and re-layouts: 19.5 us -> none  [the longest x2 15.6 us: local(): jnp.flip(jnp.cumsum(jnp.flip(press_adjoint, axis=1), axis=1), axis=1)]
    ppermute x8 -> x0, starting transfers between devices: 17.3 us -> none  [the longest x4 12.2 us: padded_2(): lax.ppermute(lax.slice_in_dim(block, block.shape[dim] - width, None, axis...]
    select_n x109 -> x0, other arithmetic: 12.8 us -> none  [the longest x46 8.51 us: select_strips(): jnp.where(valid[:, None, None], strip, held[..., offset:offset + length])]
    mul x14 -> x0, other arithmetic: 12 us -> none  [the longest x7 5.95 us: laplace(): values = shifted_sum(wet * field, weighted_halo)]
  transfers between devices with their start and end apart: 8 -> 0, of which waited for: 0 -> 0; matrix products, arithmetic and copies ran while one was open for 13% -> 0% of each run, Pallas kernels for 0% -> 0%
where the time goes in v1:
time: 50 us; the launch traced here: 49.6 us
  Pallas kernels  37.1 us (74%)
  local copies, waits for them, and re-layouts  11.9 us (24%)
  between operations  0.66 us (1%)
    pallas_call x1, Pallas kernels, local(): pl.pallas_call(functools.partial(kernel, inner, outer, depth, rows * dept...  37.1 us
    unnamed x26, local copies, waits for them, and re-layouts  11.9 us

profile of v1, /device:TPU:0, one launch (start us, length us, event | category | flops | bytes accessed | tf_op | source)
XLA Modules:
  0.0 49.6 jit_solution(9000430568722049963)
XLA Ops:
  0.6 0.0 copy-start
  0.6 0.9 %copy-done = f32[1,8,6300]{2,1,0:T(8,128)S(1)} copy-done((f32[1,8,6300]{2,1,0:T(8,128)S(1)}, f32[1,8,6300]{2,1,0:T(8,128)}, u32[]{:S(2)}) %copy-start) | copy-done | bytes 201624
  1.6 0.0 copy-start.1
  1.6 0.9 %copy-done.1 = f32[1,8,6300]{2,1,0:T(8,128)S(1)} copy-done((f32[1,8,6300]{2,1,0:T(8,128)S(1)}, f32[1,8,6300]{2,1,0:T(8,128)}, u32[]{:S(2)}) %copy-start.1) | copy-done | bytes 201624
  2.5 0.0 copy-start.2
  2.5 0.9 %copy-done.2 = f32[1,8,6300]{2,1,0:T(8,128)S(1)} copy-done((f32[1,8,6300]{2,1,0:T(8,128)S(1)}, f32[1,8,6300]{2,1,0:T(8,128)}, u32[]{:S(2)}) %copy-start.2) | copy-done | bytes 201624
  3.4 0.0 copy-start.3
  3.4 0.9 %copy-done.3 = f32[1,8,6300]{2,1,0:T(8,128)S(1)} copy-done((f32[1,8,6300]{2,1,0:T(8,128)S(1)}, f32[1,8,6300]{2,1,0:T(8,128)}, u32[]{:S(2)}) %copy-start.3) | copy-done | bytes 201624
  4.4 0.0 copy-start.4
  4.4 0.9 %copy-done.4 = f32[1,8,6300]{2,1,0:T(8,128)S(1)} copy-done((f32[1,8,6300]{2,1,0:T(8,128)S(1)}, f32[1,8,6300]{2,1,0:T(8,128)}, u32[]{:S(2)}) %copy-start.4) | copy-done | bytes 201624
  5.3 0.0 copy-start.5
  5.3 0.9 %copy-done.5 = f32[1,8,6300]{2,1,0:T(8,128)S(1)} copy-done((f32[1,8,6300]{2,1,0:T(8,128)S(1)}, f32[1,8,6300]{2,1,0:T(8,128)}, u32[]{:S(2)}) %copy-start.5) | copy-done | bytes 201624
  6.2 0.0 copy-start.6
  6.2 0.9 %copy-done.6 = f32[1,8,6300]{2,1,0:T(8,128)S(1)} copy-done((f32[1,8,6300]{2,1,0:T(8,128)S(1)}, f32[1,8,6300]{2,1,0:T(8,128)}, u32[]{:S(2)}) %copy-start.6) | copy-done | bytes 201624
  7.1 0.0 copy-start.7
  7.2 0.7 %copy-done.7 = s32[1,6300]{1,0:T(1,128)S(1)} copy-done((s32[1,6300]{1,0:T(1,128)S(1)}, s32[1,6300]{1,0:T(1,128)}, u32[]{:S(2)}) %copy-start.7) | copy-done | bytes 25224
  7.9 0.0 copy-start.8
  7.9 0.7 %copy-done.8 = s32[1,4]{1,0:T(1,128)S(1)} copy-done((s32[1,4]{1,0:T(1,128)S(1)}, s32[1,4]{1,0:T(1,128)}, u32[]{:S(2)}) %copy-start.8) | copy-done | bytes 40
  8.5 0.0 copy-start.9
  8.5 0.7 %copy-done.9 = s32[1,4]{1,0:T(1,128)S(1)} copy-done((s32[1,4]{1,0:T(1,128)S(1)}, s32[1,4]{1,0:T(1,128)}, u32[]{:S(2)}) %copy-start.9) | copy-done | bytes 40
  9.2 0.0 copy-start.10
  9.2 0.7 %copy-done.10 = s32[1,4]{1,0:T(1,128)S(1)} copy-done((s32[1,4]{1,0:T(1,128)S(1)}, s32[1,4]{1,0:T(1,128)}, u32[]{:S(2)}) %copy-start.10) | copy-done | bytes 40
  9.9 37.1 %shard_map.138 = (f32[1,8,6300]{2,1,0:T(8,128)S(1)}, f32[1,8,6300]{2,1,0:T(8,128)S(1)}, f32[1,8,6300]{2,1,0:T(8,128)S(1)}, f32[1,8,6300]{2,1,0:T(8,128)S(1)}) custom-call(f32[1,8,6300]{2,1,0:T(8,128)S(1)} %copy-done, f32[1,8,6300]{2,1,0:T(8,128)S(1)} %copy-done.1, f32[1,8,6300]{2,1,0:T(8,128)S(1)} %copy-done.2, f32[1,8,6300]{2,1,0:T(8,128)S(1)} %copy-done.3, ...), custom_call_target="tpu_custom_call" | custom-call | tf_op jit(solution)/shard_map/pallas_call | solution.py:283
  46.9 0.7 %copy.19 = f32[1,8,6300]{2,1,0:T(8,128)} copy(f32[1,8,6300]{2,1,0:T(8,128)S(1)} %get-tuple-element.8) | data formatting | bytes 403200
  47.6 0.7 %copy.20 = f32[1,8,6300]{2,1,0:T(8,128)} copy(f32[1,8,6300]{2,1,0:T(8,128)S(1)} %get-tuple-element.9) | data formatting | bytes 403200
  48.3 0.7 %copy.21 = f32[1,8,6300]{2,1,0:T(8,128)} copy(f32[1,8,6300]{2,1,0:T(8,128)S(1)} %get-tuple-element.10) | data formatting | bytes 403200
  49.0 0.7 %copy.22 = f32[1,8,6300]{2,1,0:T(8,128)} copy(f32[1,8,6300]{2,1,0:T(8,128)S(1)} %get-tuple-element.11) | data formatting | bytes 403200
Async XLA Ops:
  0.6 0.9 %copy-start = (f32[1,8,6300]{2,1,0:T(8,128)S(1)}, f32[1,8,6300]{2,1,0:T(8,128)}, u32[]{:S(2)}) copy-start(f32[1,8,6300]{2,1,0:T(8,128)} %mom_ref.1) | copy-start | bytes 604804
  1.6 0.9 %copy-start.1 = (f32[1,8,6300]{2,1,0:T(8,128)S(1)}, f32[1,8,6300]{2,1,0:T(8,128)}, u32[]{:S(2)}) copy-start(f32[1,8,6300]{2,1,0:T(8,128)} %tra_ref.1) | copy-start | bytes 604804
  2.5 0.9 %copy-start.2 = (f32[1,8,6300]{2,1,0:T(8,128)S(1)}, f32[1,8,6300]{2,1,0:T(8,128)}, u32[]{:S(2)}) copy-start(f32[1,8,6300]{2,1,0:T(8,128)} %mdif_ref.1) | copy-start | bytes 604804
  3.4 0.9 %copy-start.3 = (f32[1,8,6300]{2,1,0:T(8,128)S(1)}, f32[1,8,6300]{2,1,0:T(8,128)}, u32[]{:S(2)}) copy-start(f32[1,8,6300]{2,1,0:T(8,128)} %tdif_ref.1) | copy-start | bytes 604804
  4.4 0.9 %copy-start.4 = (f32[1,8,6300]{2,1,0:T(8,128)S(1)}, f32[1,8,6300]{2,1,0:T(8,128)}, u32[]{:S(2)}) copy-start(f32[1,8,6300]{2,1,0:T(8,128)} %mix_ref.1) | copy-start | bytes 604804
  5.3 0.9 %copy-start.5 = (f32[1,8,6300]{2,1,0:T(8,128)S(1)}, f32[1,8,6300]{2,1,0:T(8,128)}, u32[]{:S(2)}) copy-start(f32[1,8,6300]{2,1,0:T(8,128)} %mcot_ref.1) | copy-start | bytes 604804
  6.2 0.9 %copy-start.6 = (f32[1,8,6300]{2,1,0:T(8,128)S(1)}, f32[1,8,6300]{2,1,0:T(8,128)}, u32[]{:S(2)}) copy-start(f32[1,8,6300]{2,1,0:T(8,128)} %tcot_ref.1) | copy-start | bytes 604804
  7.1 0.7 %copy-start.7 = (s32[1,6300]{1,0:T(1,128)S(1)}, s32[1,6300]{1,0:T(1,128)}, u32[]{:S(2)}) copy-start(s32[1,6300]{1,0:T(1,128)} %wet_ref.1) | copy-start | bytes 75604
  7.9 0.7 %copy-start.8 = (s32[1,4]{1,0:T(1,128)S(1)}, s32[1,4]{1,0:T(1,128)}, u32[]{:S(2)}) copy-start(s32[1,4]{1,0:T(1,128)} %nb_ref.1) | copy-start | bytes 52
  8.5 0.7 %copy-start.9 = (s32[1,4]{1,0:T(1,128)S(1)}, s32[1,4]{1,0:T(1,128)}, u32[]{:S(2)}) copy-start(s32[1,4]{1,0:T(1,128)} %se_ref.1) | copy-start | bytes 52
  9.2 0.7 %copy-start.10 = (s32[1,4]{1,0:T(1,128)S(1)}, s32[1,4]{1,0:T(1,128)}, u32[]{:S(2)}) copy-start(s32[1,4]{1,0:T(1,128)} %fl_ref.1) | copy-start | bytes 52

commit v2 on v1

--- a/solution.py
+++ b/solution.py
@@ -26,10 +26,11 @@
 
 def kernel(
     inner, outer, depth, levels_all,
+    mom_hbm, tra_hbm, mdif_hbm, tdif_hbm, mix_hbm, wet_hbm, nb_hbm, se_hbm, fl_hbm, mcot_hbm, tcot_hbm,
+    mom_out, tra_out, mgrad_out, tgrad_out,
     mom_ref, tra_ref, mdif_ref, tdif_ref, mix_ref, wet_ref, nb_ref, se_ref, fl_ref, mcot_ref, tcot_ref,
-    mom_out, tra_out, mgrad_out, tgrad_out,
     table, tables, tables_s, grid, gath_0, gath_1, part, halo, edge_s, edge_r, carry_s, carry_r,
-    tab_send, tab_recv, tab_local, g_send, g_recv, h_send, h_recv, e_send, e_recv, c_send, c_recv,
+    in_sem, tab_send, tab_recv, tab_local, g_send, g_recv, h_send, h_recv, e_send, e_recv, c_send, c_recv,
 ):
     me = lax.axis_index("tiles")
     d = lax.axis_index("depth")
@@ -48,6 +49,15 @@
     def in_depth(o):
         return {"tiles": me, "depth": lax.rem(d + o, depth)}
 
+    fetched = []
+    for k, (src, dst) in enumerate((
+        (nb_hbm, nb_ref), (se_hbm, se_ref), (fl_hbm, fl_ref), (wet_hbm, wet_ref), (mcot_hbm, mcot_ref),
+        (tdif_hbm, tdif_ref), (tcot_hbm, tcot_ref), (tra_hbm, tra_ref), (mom_hbm, mom_ref), (mdif_hbm, mdif_ref),
+        (mix_hbm, mix_ref),
+    )):
+        fetched.append(pltpu.make_async_copy(src, dst, in_sem.at[k]))
+        fetched[-1].start()
+    grid[...] = jnp.zeros_like(grid)
     barrier = pltpu.get_barrier_semaphore()
     for count, where_to in ((inner, in_inner), (outer, in_outer), (depth, in_depth)):
         for o in range(1, count):
@@ -64,6 +74,8 @@
         started.append(copy)
         return copy
 
+    for copy in fetched[:3]:
+        copy.wait()
     table[...] = jnp.zeros_like(table)
     table[0:1, 0:4] = nb_ref[...]
     table[1:2, 0:4] = se_ref[...]
@@ -81,12 +93,20 @@
     on_edge = jnp.where(at_west | at_east, 1.0, 0.0)
     lane = lax.broadcasted_iota(jnp.int32, (total, LANES), 1)
     odd = lax.rem(lane, 2) == 1
+    odd6 = lax.rem(lax.broadcasted_iota(jnp.int32, (6 * rows, LANES), 1), 2) == 1
     level = lax.broadcasted_iota(jnp.int32, (rows, CELLS), 0)
+    level8 = lax.broadcasted_iota(jnp.int32, (rows, LANES), 0)
+    tail = jnp.zeros((total, LANES), jnp.float32)
+    for j in range(NJ - 64):
+        for x in (NI * j % LANES, (NI * j + NI - 1) % LANES):
+            tail = jnp.where(lane == x, 1.0, tail)
 
     r0 = lax.broadcasted_iota(jnp.int32, (LANES, LANES), 0)
     r1 = lax.broadcasted_iota(jnp.int32, (LANES, LANES), 1)
     rev_i = jnp.where(r0 + r1 == NI - 1, 1.0, 0.0)
 
+    for copy in fetched[3:]:
+        copy.wait()
     wet = jnp.broadcast_to(wet_ref[...].astype(jnp.float32), (rows, CELLS))
     mdif, tdif, mix = mdif_ref[0], tdif_ref[0], mix_ref[0]
 
@@ -100,7 +120,6 @@
             k *= 2
         return x
 
-    grid[...] = jnp.zeros_like(grid)
     m, s, lm, lt = mom_ref[0], tra_ref[0], mcot_ref[0], tcot_ref[0]
     has_above = jnp.where(d > 0, 1.0, 0.0)
     has_below = jnp.where(d < depth - 1, 1.0, 0.0)
@@ -129,17 +148,30 @@
         grid[3 * rows : 4 * rows, LO:HI] = wet * u
         grid[4 * rows : 5 * rows, LO:HI] = jnp.where(level == 0, wet, jnp.where(level == 1, wet * t_sum, 0.0))
 
-        gath[member, 0] = roll(grid[:, WIDTH - 2 * LANES : WIDTH], -(HI - NI - (WIDTH - 2 * LANES)))[:, :LANES]
-        gath[member, 1] = grid[:, LO : LO + LANES]
+        tail_at = WIDTH - 2 * LANES
+        north = roll(grid[:, tail_at:WIDTH], -(HI - NI - tail_at))[:, :LANES]
+        south = grid[:, LO : LO + LANES]
+        last = None
         for g in range(5):
             span = slice(g * rows, (g + 1) * rows)
-            for part_of, (a, b) in enumerate(((1, 1 + FIRST), (1 + FIRST, CHUNKS))):
+            packed = []
+            for a, b in ((1, 1 + FIRST), (1 + FIRST, CHUNKS)):
                 acc = None
                 for v in range(a, b):
                     cut = slice(v * LANES, (v + 1) * LANES)
                     piece = grid[span, cut] * on_edge[:, cut]
                     acc = piece if acc is None else acc + piece
-                gath[member, 2 + part_of, span] = acc
+                packed.append(acc)
+            last = packed[1] if g == 0 else last + roll(packed[1], 2 * g)
+            if g < 4:
+                gath[member, g] = north[span]
+                gath[member, 4 + g] = south[span]
+                gath[member, 8 + g] = packed[0]
+            else:
+                gath[member, 12] = jnp.where(level8 < 2, north[span], 0.0) + roll(
+                    jnp.where(level8 < 2, south[span], 0.0), 2, 0
+                ) + roll(packed[0], 4, 0)
+        gath[member, 13] = last
         copies = [
             send(gath.at[member], gath.at[member], g_send.at[r, o], g_recv.at[r, o], in_inner(o))
             for o in range(1, inner)
@@ -162,31 +194,42 @@
                 return lax.rem(known, inner), edge, jnp.where(here, 1.0, 0.0)
 
             result = []
+            odds = []
             for direction in range(2):
                 tile, edge, here = source(direction)
-                result.append(gath[tile, jnp.where(edge == 0, 0, 1)] * here)
+                edge = jnp.where(edge == 0, 0, 1)
+                result.append((gath[tile, pl.ds(4 * edge, 4)] * here).reshape(4 * rows, LANES))
+                two = gath[tile, 12] * here
+                second = edge.astype(jnp.float32)
+                odds.append(roll(two, -2, 0) * second + two * (1.0 - second))
             east, east_edge, east_here = source(2)
             west, west_edge, west_here = source(3)
             east_turn = jnp.where(east_edge == 3, 1.0, 0.0)
             west_turn = jnp.where(west_edge == 2, 1.0, 0.0)
-            for k in (2, 3):
-                e = gath[east, k]
-                e = (roll(e, NI - 1) * east_turn + e * (1.0 - east_turn)) * east_here
-                w = gath[west, k]
-                w = (roll(w, 1 - NI) * west_turn + w * (1.0 - west_turn)) * west_here
-                result.append(jnp.where(odd, e, w))
-            return result
+            e = gath[east, 8:14].reshape(6 * rows, LANES)
+            e = (roll(e, NI - 1) * east_turn + e * (1.0 - east_turn)) * east_here
+            w = gath[west, 8:14].reshape(6 * rows, LANES)
+            w = (roll(w, 1 - NI) * west_turn + w * (1.0 - west_turn)) * west_here
+            side = jnp.where(odd6, e, w)
+            mid = side[4 * rows : 5 * rows]
+            mid = jnp.where(level8 < 2, odds[0], jnp.where(level8 < 4, roll(odds[1], 2, 0), mid))
+            return jnp.concatenate([result[0], result[1], side[: 4 * rows], mid, side[5 * rows :]], axis=0)
 
         copies = []
         for o in range(1, outer):
-            for k, strip in enumerate(strips_for(lax.rem(group + o, outer))):
-                part[r, o, k] = strip
+            part[r, o] = strips_for(lax.rem(group + o, outer)).reshape(14, rows, LANES)
             copies.append(send(part.at[r, o], halo.at[r, o], h_send.at[r, o], h_recv.at[r, o], in_outer(o)))
-        strips = strips_for(group)
+        merged = strips_for(group)
         for o in range(1, outer):
             copies[o - 1].wait_recv()
-            for k in range(4):
-                strips[k] = strips[k] + halo[r, o, k]
+            merged = merged + halo[r, o].reshape(14 * rows, LANES)
+        mid, last = merged[12 * rows : 13 * rows], merged[13 * rows :]
+        strips = [
+            jnp.concatenate([merged[: 4 * rows], mid], axis=0),
+            jnp.concatenate([merged[4 * rows : 8 * rows], roll(mid, -2, 0)], axis=0),
+            jnp.concatenate([merged[8 * rows : 12 * rows], roll(mid, -4, 0)], axis=0),
+            jnp.where(tail > 0.5, jnp.concatenate([roll(last, -2 * g) for g in range(5)], axis=0), 0.0),
+        ]
 
         flip = [jnp.where(tables_s[group, 2, k] == 1, 1.0, 0.0) for k in range(4)]
         dot = functools.partial(jnp.dot, precision=EXACT, preferred_element_type=jnp.float32)
@@ -196,10 +239,6 @@
         aim = jnp.where(both, NI * (NJ - 1) % LANES, (NI * (NJ - 1) + 2 * (NI - 1)) % LANES)
         turn = jnp.where(lax.rem(r0 + r1 + LANES * 4 - aim, LANES) == 0, 1.0, 0.0)
         one, two = dot(strips[2], turn), dot(strips[3], turn)
-        tail = jnp.zeros((total, LANES), jnp.float32)
-        for j in range(NJ - 64):
-            for x in (NI * j % LANES, (NI * j + NI - 1) % LANES):
-                tail = jnp.where(lane == x, 1.0, tail)
         turned_one = jnp.where(tail > 0.5, two, one)
         turned_two = jnp.where(tail > 0.5, one, 0.0)
         ew_flip = jnp.where(odd, flip[2], flip[3])
@@ -268,6 +307,15 @@
         copy.wait_send()
 
 
+def write_out(*refs):
+    sems = refs[8]
+    copies = [pltpu.make_async_copy(refs[k], refs[4 + k], sems.at[k]) for k in range(4)]
+    for copy in copies:
+        copy.start()
+    for copy in copies:
+        copy.wait()
+
+
 def solution(mesh):
     tiles, depth = mesh.shape["tiles"], mesh.shape["depth"]
     inner = max(k for k in range(1, tiles + 1) if tiles % k == 0 and k * k <= tiles)
@@ -280,34 +328,43 @@
         f32 = jnp.float32
         shape = jax.ShapeDtypeStruct(args[0].shape, f32)
         vmem = pl.BlockSpec(memory_space=pltpu.VMEM)
-        return pl.pallas_call(
+        hbm = pl.BlockSpec(memory_space=pltpu.MemorySpace.HBM)
+        results = pl.pallas_call(
             functools.partial(kernel, inner, outer, depth, rows * depth),
             out_shape=(shape,) * 4,
-            in_specs=[vmem] * 11,
+            in_specs=[hbm] * 11,
             out_specs=(vmem,) * 4,
             scratch_shapes=[
+                *[pltpu.VMEM(a.shape, a.dtype) for a in args],
                 pltpu.VMEM((8, LANES), jnp.int32),
                 pltpu.VMEM((outer, 8, LANES), jnp.int32),
                 pltpu.SMEM((outer, 8, LANES), jnp.int32),
                 pltpu.VMEM((total, WIDTH), f32),
-                pltpu.VMEM((inner, 4, total, LANES), f32),
-                pltpu.VMEM((inner, 4, total, LANES), f32),
-                pltpu.VMEM((2, outer, 4, total, LANES), f32),
-                pltpu.VMEM((2, outer, 4, total, LANES), f32),
+                pltpu.VMEM((inner, 14, rows, LANES), f32),
+                pltpu.VMEM((inner, 14, rows, LANES), f32),
+                pltpu.VMEM((2, outer, 14, rows, LANES), f32),
+                pltpu.VMEM((2, outer, 14, rows, LANES), f32),
                 pltpu.VMEM((2, 2, 2, CELLS), f32),
                 pltpu.VMEM((2, 2, 2, CELLS), f32),
                 pltpu.VMEM((2, 2, CELLS), f32),
                 pltpu.VMEM((2, depth, 2, CELLS), f32),
-                dma((outer,)), dma((outer,)), dma(()),
+                dma((11,)), dma((outer,)), dma((outer,)), dma(()),
                 dma((2, inner)), dma((2, inner)),
                 dma((2, outer)), dma((2, outer)),
                 dma((2, 2)), dma((2, 2)),
                 dma((2, depth)), dma((2, depth)),
             ],
             compiler_params=pltpu.CompilerParams(
-                collective_id=0, has_side_effects=True, vmem_limit_bytes=48 * 1024 * 1024
+                collective_id=0, has_side_effects=True, vmem_limit_bytes=62 * 1024 * 1024
             ),
         )(*args)
+        return pl.pallas_call(
+            write_out,
+            out_shape=(shape,) * 4,
+            in_specs=[pl.BlockSpec(memory_space=pl.ANY)] * 4,
+            out_specs=(hbm,) * 4,
+            scratch_shapes=[dma((4,))],
+        )(*results)
 
     whole = P("tiles", "depth", None)
     flat = P("tiles", None)

time: 50 us -> 58.6 us (1.17)
  Pallas kernels: 37.1 us -> 57.8 us
  local copies, waits for them, and re-layouts: 11.9 us -> 0 us
    pallas_call x0 -> x1, Pallas kernels: none -> 26 us  [local(): pl.pallas_call(write_out, out_shape=(shape,) * 4, in_specs=[pl.BlockSpec(...]
    unnamed x26 -> x0, local copies, waits for them, and re-layouts: 11.9 us -> none
    pallas_call x1, Pallas kernels: 37.1 us -> 31.8 us  [local(): pl.pallas_call(functools.partial(kernel, inner, outer, depth, rows * dept...]
where the time goes in v2:
time: 58.6 us; the launch traced here: 58.4 us
  Pallas kernels  57.8 us (99%)
  between operations  0.64 us (1%)
    pallas_call x1, Pallas kernels, local(): pl.pallas_call(functools.partial(kernel, inner, outer, depth, rows * dept...  31.8 us
    pallas_call x1, Pallas kernels, local(): pl.pallas_call(write_out, out_shape=(shape,) * 4, in_specs=[pl.BlockSpec(...  26 us

profile of v2, /device:TPU:0, one launch (start us, length us, event | category | flops | bytes accessed | tf_op | source)
XLA Modules:
  0.0 58.4 jit_solution(4366230874442184588)
XLA Ops:
  0.6 31.8 %shard_map.138 = (f32[1,8,6300]{2,1,0:T(8,128)}, f32[1,8,6300]{2,1,0:T(8,128)}, f32[1,8,6300]{2,1,0:T(8,128)}, f32[1,8,6300]{2,1,0:T(8,128)}) custom-call(f32[1,8,6300]{2,1,0:T(8,128)} %mom_hbm.1, f32[1,8,6300]{2,1,0:T(8,128)} %tra_hbm.1, f32[1,8,6300]{2,1,0:T(8,128)} %mdif_hbm.1, f32[1,8,6300]{2,1,0:T(8,128)} %tdif_hbm.1, f32[1,8,6300]{2,1,0:T(8,128)} %mix_hbm.1, ...), custom_call_target="tpu_custom_call" | custom-call | tf_op jit(solution)/shard_map/pallas_call | solution.py:332
  32.5 26.0 %shard_map.139 = (f32[1,8,6300]{2,1,0:T(8,128)}, f32[1,8,6300]{2,1,0:T(8,128)}, f32[1,8,6300]{2,1,0:T(8,128)}, f32[1,8,6300]{2,1,0:T(8,128)}) custom-call(f32[1,8,6300]{2,1,0:T(8,128)} %get-tuple-element.8.refs_0_, f32[1,8,6300]{2,1,0:T(8,128)} %get-tuple-element.9.refs_1_, f32[1,8,6300]{2,1,0:T(8,128)} %get-tuple-element.10.refs_2_, ...), custom_call_target="tpu_custom_call" | custom-call | tf_op jit(solution)/shard_map/pallas_call | solution.py:361

commit v3 on v2

--- a/solution.py
+++ b/solution.py
@@ -308,11 +308,15 @@
 
 
 def write_out(*refs):
-    sems = refs[8]
-    copies = [pltpu.make_async_copy(refs[k], refs[4 + k], sems.at[k]) for k in range(4)]
-    for copy in copies:
+    sources, targets, staged, sems = refs[:4], refs[4:8], refs[8:12], refs[12]
+    reads = [pltpu.make_async_copy(sources[k], staged[k], sems.at[0, k]) for k in range(4)]
+    writes = [pltpu.make_async_copy(staged[k], targets[k], sems.at[1, k]) for k in range(4)]
+    for copy in reads:
         copy.start()
-    for copy in copies:
+    for read, write in zip(reads, writes):
+        read.wait()
+        write.start()
+    for copy in writes:
         copy.wait()
 
 
@@ -363,7 +367,8 @@
             out_shape=(shape,) * 4,
             in_specs=[pl.BlockSpec(memory_space=pl.ANY)] * 4,
             out_specs=(hbm,) * 4,
-            scratch_shapes=[dma((4,))],
+            scratch_shapes=[pltpu.VMEM(shape.shape, f32)] * 4 + [dma((2, 4))],
+            compiler_params=pltpu.CompilerParams(vmem_limit_bytes=62 * 1024 * 1024),
         )(*results)
 
     whole = P("tiles", "depth", None)

time: 58.6 us -> 34.6 us (0.59)
  Pallas kernels: 57.8 us -> 33.8 us
    pallas_call x1, Pallas kernels: 26 us -> 1.98 us  [local(): pl.pallas_call(write_out, out_shape=(shape,) * 4, in_specs=[pl.BlockSpec(...]
where the time goes in v3:
time: 34.6 us; the launch traced here: 34.5 us
  Pallas kernels  33.8 us (98%)
  between operations  0.64 us (2%)
    pallas_call x1, Pallas kernels, local(): pl.pallas_call(functools.partial(kernel, inner, outer, depth, rows * dept...  31.8 us
    pallas_call x1, Pallas kernels, local(): pl.pallas_call(write_out, out_shape=(shape,) * 4, in_specs=[pl.BlockSpec(...  1.98 us

profile of v3, /device:TPU:0, one launch (start us, length us, event | category | flops | bytes accessed | tf_op | source)
XLA Modules:
  0.0 34.5 jit_solution(4576905947837488950)
XLA Ops:
  0.6 31.8 %shard_map.138 = (f32[1,8,6300]{2,1,0:T(8,128)}, f32[1,8,6300]{2,1,0:T(8,128)}, f32[1,8,6300]{2,1,0:T(8,128)}, f32[1,8,6300]{2,1,0:T(8,128)}) custom-call(f32[1,8,6300]{2,1,0:T(8,128)} %mom_hbm.1, f32[1,8,6300]{2,1,0:T(8,128)} %tra_hbm.1, f32[1,8,6300]{2,1,0:T(8,128)} %mdif_hbm.1, f32[1,8,6300]{2,1,0:T(8,128)} %tdif_hbm.1, f32[1,8,6300]{2,1,0:T(8,128)} %mix_hbm.1, ...), custom_call_target="tpu_custom_call" | custom-call | tf_op jit(solution)/shard_map/pallas_call | solution.py:336
  32.5 2.0 %shard_map.139 = (f32[1,8,6300]{2,1,0:T(8,128)}, f32[1,8,6300]{2,1,0:T(8,128)}, f32[1,8,6300]{2,1,0:T(8,128)}, f32[1,8,6300]{2,1,0:T(8,128)}) custom-call(f32[1,8,6300]{2,1,0:T(8,128)} %get-tuple-element.8.refs_0_, f32[1,8,6300]{2,1,0:T(8,128)} %get-tuple-element.9.refs_1_, f32[1,8,6300]{2,1,0:T(8,128)} %get-tuple-element.10.refs_2_, ...), custom_call_target="tpu_custom_call" | custom-call | tf_op jit(solution)/shard_map/pallas_call | solution.py:365

commit v4 on v3

--- a/solution.py
+++ b/solution.py
@@ -29,7 +29,7 @@
     mom_hbm, tra_hbm, mdif_hbm, tdif_hbm, mix_hbm, wet_hbm, nb_hbm, se_hbm, fl_hbm, mcot_hbm, tcot_hbm,
     mom_out, tra_out, mgrad_out, tgrad_out,
     mom_ref, tra_ref, mdif_ref, tdif_ref, mix_ref, wet_ref, nb_ref, se_ref, fl_ref, mcot_ref, tcot_ref,
-    table, tables, tables_s, grid, gath_0, gath_1, part, halo, edge_s, edge_r, carry_s, carry_r,
+    table, tables, tables_s, grid, base, gath_0a, gath_0b, gath_1a, gath_1b, part, halo, edge_s, edge_r, carry_s, carry_r,
     in_sem, tab_send, tab_recv, tab_local, g_send, g_recv, h_send, h_recv, e_send, e_recv, c_send, c_recv,
 ):
     me = lax.axis_index("tiles")
@@ -62,7 +62,6 @@
     for count, where_to in ((inner, in_inner), (outer, in_outer), (depth, in_depth)):
         for o in range(1, count):
             pl.semaphore_signal(barrier, inc=1, device_id=where_to(o), device_id_type=MESH)
-    pl.semaphore_wait(barrier, inner + outer + depth - 3)
 
     started = []
 
@@ -81,10 +80,6 @@
     table[1:2, 0:4] = se_ref[...]
     table[2:3, 0:4] = fl_ref[...]
     tables[group] = table[...]
-    table_copies = [
-        send(table, tables.at[group], tab_send.at[o], tab_recv.at[o], in_outer(o)) for o in range(1, outer)
-    ]
-
     pos = (lax.broadcasted_iota(jnp.int32, (8, WIDTH), 1) - LO).astype(jnp.float32)
     col = pos - NI * jnp.floor((pos + 0.5) * (1.0 / NI))
     inside = (pos > -0.5) & (pos < CELLS - 0.5)
@@ -93,7 +88,6 @@
     on_edge = jnp.where(at_west | at_east, 1.0, 0.0)
     lane = lax.broadcasted_iota(jnp.int32, (total, LANES), 1)
     odd = lax.rem(lane, 2) == 1
-    odd6 = lax.rem(lax.broadcasted_iota(jnp.int32, (6 * rows, LANES), 1), 2) == 1
     level = lax.broadcasted_iota(jnp.int32, (rows, CELLS), 0)
     level8 = lax.broadcasted_iota(jnp.int32, (rows, LANES), 0)
     tail = jnp.zeros((total, LANES), jnp.float32)
@@ -123,30 +117,19 @@
     m, s, lm, lt = mom_ref[0], tra_ref[0], mcot_ref[0], tcot_ref[0]
     has_above = jnp.where(d > 0, 1.0, 0.0)
     has_below = jnp.where(d < depth - 1, 1.0, 0.0)
-    weights = None
 
     for r in range(2):
-        gath = (gath_0, gath_1)[r]
+        gath_a, gath_b = ((gath_0a, gath_0b), (gath_1a, gath_1b))[r]
         mixed = mix * lt
-        edge_copies = []
-        if depth > 1:
-            edge_s[r, 0, 0:1] = s[rows - 1 : rows]
-            edge_s[r, 0, 1:2] = mixed[rows - 1 : rows]
-            edge_s[r, 1, 0:1] = s[0:1]
-            edge_s[r, 1, 1:2] = mixed[0:1]
-            for i, o in ((0, 1), (1, depth - 1)):
-                edge_copies.append(
-                    send(edge_s.at[r, i], edge_r.at[r, i], e_send.at[r, i], e_recv.at[r, i], in_depth(o))
-                )
         back = running(lm, False)
         u = tdif * lt + press * back
         w_m = mdif * lm
         t_sum = press * back[0:1]
         grid[0:rows, LO:HI] = wet * m
         grid[rows : 2 * rows, LO:HI] = wet * s
-        grid[2 * rows : 3 * rows, LO:HI] = wet * w_m
-        grid[3 * rows : 4 * rows, LO:HI] = wet * u
-        grid[4 * rows : 5 * rows, LO:HI] = jnp.where(level == 0, wet, jnp.where(level == 1, wet * t_sum, 0.0))
+        grid[2 * rows : 3 * rows, LO:HI] = jnp.where(level == 0, wet, jnp.where(level == 1, wet * t_sum, 0.0))
+        grid[3 * rows : 4 * rows, LO:HI] = wet * w_m
+        grid[4 * rows : 5 * rows, LO:HI] = wet * u
 
         tail_at = WIDTH - 2 * LANES
         north = roll(grid[:, tail_at:WIDTH], -(HI - NI - tail_at))[:, :LANES]
@@ -163,29 +146,59 @@
                     acc = piece if acc is None else acc + piece
                 packed.append(acc)
             last = packed[1] if g == 0 else last + roll(packed[1], 2 * g)
-            if g < 4:
-                gath[member, g] = north[span]
-                gath[member, 4 + g] = south[span]
-                gath[member, 8 + g] = packed[0]
-            else:
-                gath[member, 12] = jnp.where(level8 < 2, north[span], 0.0) + roll(
+            if g == 2:
+                gath_a[member, 6] = jnp.where(level8 < 2, north[span], 0.0) + roll(
                     jnp.where(level8 < 2, south[span], 0.0), 2, 0
                 ) + roll(packed[0], 4, 0)
-        gath[member, 13] = last
-        copies = [
-            send(gath.at[member], gath.at[member], g_send.at[r, o], g_recv.at[r, o], in_inner(o))
-            for o in range(1, inner)
+            else:
+                gath, k = (gath_a, g) if g < 2 else (gath_b, g - 3)
+                gath[member, k] = north[span]
+                gath[member, 2 + k] = south[span]
+                gath[member, 4 + k] = packed[0]
+        gath_a[member, 7] = last
+
+        if r == 0:
+            pl.semaphore_wait(barrier, inner + outer + depth - 3)
+            table_copies = [
+                send(table, tables.at[group], tab_send.at[o], tab_recv.at[o], in_outer(o)) for o in range(1, outer)
+            ]
+        first_copies = [
+            [
+                send(gath.at[member], gath.at[member], g_send.at[r, h, o], g_recv.at[r, h, o], in_inner(o))
+                for o in range(1, inner)
+            ]
+            for h, gath in enumerate((gath_a, gath_b))
         ]
+        edge_copies = []
+        if depth > 1:
+            edge_s[r, 0, 0:1] = s[rows - 1 : rows]
+            edge_s[r, 0, 1:2] = mixed[rows - 1 : rows]
+            edge_s[r, 1, 0:1] = s[0:1]
+            edge_s[r, 1, 1:2] = mixed[0:1]
+            for i, o in ((0, 1), (1, depth - 1)):
+                edge_copies.append(
+                    send(edge_s.at[r, i], edge_r.at[r, i], e_send.at[r, i], e_recv.at[r, i], in_depth(o))
+                )
+
+        def inside_sums(g):
+            span = slice(g * rows, (g + 1) * rows)
+            x = grid[span, :]
+            east = jnp.where(at_east, 0.0, roll(x, -1))
+            west = jnp.where(at_west, 0.0, roll(x, 1))
+            base[span, :] = roll(x, -NI) + roll(x, NI) + east + west
+
+        inside_sums(0)
+        inside_sums(1)
         if r == 0:
             for copy in table_copies:
                 copy.wait_recv()
             local = pltpu.make_async_copy(tables, tables_s, tab_local)
             local.start()
             local.wait()
-        for copy in copies:
-            copy.wait_recv()
-
-        def strips_for(target):
+
+        def strips_for(target, h):
+            gath = (gath_a, gath_b)[h]
+
             def source(direction):
                 tile = tables_s[target, 0, direction]
                 edge = tables_s[target, 1, direction]
@@ -198,71 +211,112 @@
             for direction in range(2):
                 tile, edge, here = source(direction)
                 edge = jnp.where(edge == 0, 0, 1)
-                result.append((gath[tile, pl.ds(4 * edge, 4)] * here).reshape(4 * rows, LANES))
-                two = gath[tile, 12] * here
-                second = edge.astype(jnp.float32)
-                odds.append(roll(two, -2, 0) * second + two * (1.0 - second))
+                result.append((gath[tile, pl.ds(2 * edge, 2)] * here).reshape(2 * rows, LANES))
+                if h == 0:
+                    two = gath[tile, 6] * here
+                    second = edge.astype(jnp.float32)
+                    odds.append(roll(two, -2, 0) * second + two * (1.0 - second))
             east, east_edge, east_here = source(2)
             west, west_edge, west_here = source(3)
             east_turn = jnp.where(east_edge == 3, 1.0, 0.0)
             west_turn = jnp.where(west_edge == 2, 1.0, 0.0)
-            e = gath[east, 8:14].reshape(6 * rows, LANES)
+            size = gath.shape[1] - 4
+            e = gath[east, 4:].reshape(size * rows, LANES)
             e = (roll(e, NI - 1) * east_turn + e * (1.0 - east_turn)) * east_here
-            w = gath[west, 8:14].reshape(6 * rows, LANES)
+            w = gath[west, 4:].reshape(size * rows, LANES)
             w = (roll(w, 1 - NI) * west_turn + w * (1.0 - west_turn)) * west_here
-            side = jnp.where(odd6, e, w)
-            mid = side[4 * rows : 5 * rows]
-            mid = jnp.where(level8 < 2, odds[0], jnp.where(level8 < 4, roll(odds[1], 2, 0), mid))
-            return jnp.concatenate([result[0], result[1], side[: 4 * rows], mid, side[5 * rows :]], axis=0)
-
-        copies = []
-        for o in range(1, outer):
-            part[r, o] = strips_for(lax.rem(group + o, outer)).reshape(14, rows, LANES)
-            copies.append(send(part.at[r, o], halo.at[r, o], h_send.at[r, o], h_recv.at[r, o], in_outer(o)))
-        merged = strips_for(group)
-        for o in range(1, outer):
-            copies[o - 1].wait_recv()
-            merged = merged + halo[r, o].reshape(14 * rows, LANES)
-        mid, last = merged[12 * rows : 13 * rows], merged[13 * rows :]
-        strips = [
-            jnp.concatenate([merged[: 4 * rows], mid], axis=0),
-            jnp.concatenate([merged[4 * rows : 8 * rows], roll(mid, -2, 0)], axis=0),
-            jnp.concatenate([merged[8 * rows : 12 * rows], roll(mid, -4, 0)], axis=0),
-            jnp.where(tail > 0.5, jnp.concatenate([roll(last, -2 * g) for g in range(5)], axis=0), 0.0),
-        ]
+            side = jnp.where(odd[: size * rows], e, w)
+            if h == 0:
+                mid = side[2 * rows : 3 * rows]
+                mid = jnp.where(level8 < 2, odds[0], jnp.where(level8 < 4, roll(odds[1], 2, 0), mid))
+                side = jnp.concatenate([side[: 2 * rows], mid, side[3 * rows :]], axis=0)
+            return jnp.concatenate(result + [side], axis=0)
+
+        spots = (slice(0, 8), slice(8, 14))
+        second_copies = []
+        for h in range(2):
+            for copy in first_copies[h]:
+                copy.wait_recv()
+            copies = []
+            for o in range(1, outer):
+                strips = strips_for(lax.rem(group + o, outer), h)
+                part[r, o, spots[h]] = strips.reshape(strips.shape[0] // rows, rows, LANES)
+                copies.append(
+                    send(
+                        part.at[r, o, spots[h]], halo.at[r, o, spots[h]],
+                        h_send.at[r, h, o], h_recv.at[r, h, o], in_outer(o),
+                    )
+                )
+            second_copies.append(copies)
+        mine = [strips_for(group, h) for h in range(2)]
+        for g in (2, 3, 4):
+            inside_sums(g)
+
+        for copy in edge_copies:
+            copy.wait_recv()
+
+        def vertical(q, which):
+            above, below = q[0:1], q[rows - 1 : rows]
+            if depth > 1:
+                above = edge_r[r, 0, which : which + 1] * has_above + above * (1.0 - has_above)
+                below = edge_r[r, 1, which : which + 1] * has_below + below * (1.0 - has_below)
+            up = jnp.where(level == 0, above, roll(q, 1, 0))
+            down = jnp.where(level == rows - 1, below, roll(q, rows - 1, 0))
+            return (up - q) + (down - q)
+
+        s_next = s + mix * vertical(s, 0) + 0.2 * m
+        lt_next = lt + vertical(mixed, 1)
+        lm_next = lm + 0.2 * lt
 
         flip = [jnp.where(tables_s[group, 2, k] == 1, 1.0, 0.0) for k in range(4)]
         dot = functools.partial(jnp.dot, precision=EXACT, preferred_element_type=jnp.float32)
-        north = dot(strips[0], rev_i) * flip[0] + strips[0] * (1.0 - flip[0])
-        south = dot(strips[1], rev_i) * flip[1] + strips[1] * (1.0 - flip[1])
         both = lax.rem(r0, 2) == 0
         aim = jnp.where(both, NI * (NJ - 1) % LANES, (NI * (NJ - 1) + 2 * (NI - 1)) % LANES)
         turn = jnp.where(lax.rem(r0 + r1 + LANES * 4 - aim, LANES) == 0, 1.0, 0.0)
-        one, two = dot(strips[2], turn), dot(strips[3], turn)
-        turned_one = jnp.where(tail > 0.5, two, one)
-        turned_two = jnp.where(tail > 0.5, one, 0.0)
-        ew_flip = jnp.where(odd, flip[2], flip[3])
-        ew_one = jnp.where(ew_flip > 0.5, turned_one, strips[2])
-        ew_two = jnp.where(ew_flip > 0.5, turned_two, strips[3])
-
-        grid[:, 0:LANES] = roll(south, LANES - NI)
-        end = WIDTH - LANES
-        grid[:, end:] = jnp.where(lane < HI - end, grid[:, end:], roll(north, HI - end))
-
-        def around(g):
-            span = slice(g * rows, (g + 1) * rows)
-            x = grid[span, :]
+
+        def receive(h):
+            merged = mine[h]
+            for o in range(1, outer):
+                second_copies[h][o - 1].wait_recv()
+                merged = merged + halo[r, o, spots[h]].reshape(merged.shape)
+            return merged
+
+        def close(strips, lo):
+            count = strips[0].shape[0]
+            here, own, parity = slice(lo, lo + count), lane[:count], odd[:count]
+            ends = tail[:count] > 0.5
+            north = dot(strips[0], rev_i) * flip[0] + strips[0] * (1.0 - flip[0])
+            south = dot(strips[1], rev_i) * flip[1] + strips[1] * (1.0 - flip[1])
+            one, two = dot(strips[2], turn), dot(strips[3], turn)
+            ew_flip = jnp.where(parity, flip[2], flip[3]) > 0.5
+            ew_one = jnp.where(ew_flip, jnp.where(ends, two, one), strips[2])
+            ew_two = jnp.where(ew_flip, jnp.where(ends, one, 0.0), strips[3])
+            base[here, LO : LO + LANES] = base[here, LO : LO + LANES] + jnp.where(own < NI, south, 0.0)
+            north = jnp.concatenate([jnp.where(own < NI, north, 0.0), jnp.zeros_like(north)], axis=1)
+            base[here, tail_at:] = base[here, tail_at:] + roll(north, HI - NI - tail_at)
+            return ew_one, ew_two
+
+        def around(g, lo, sides):
+            span = slice(g * rows - lo, (g + 1) * rows - lo)
             side = jnp.concatenate(
-                [ew_one[span]] * (1 + FIRST) + [ew_two[span]] * (CHUNKS - 1 - FIRST), axis=1
+                [sides[0][span]] * (1 + FIRST) + [sides[1][span]] * (CHUNKS - 1 - FIRST), axis=1
             )
-            east = jnp.where(at_east, side, roll(x, -1))
-            west = jnp.where(at_west, side, roll(x, 1))
-            return (roll(x, -NI) + roll(x, NI) + east + west)[:, LO:HI]
-
-        extra = around(4)
+            return (base[g * rows : (g + 1) * rows, :] + side * on_edge)[:, LO:HI]
+
+        got = receive(0)
+        mid, last = got[6 * rows : 7 * rows], got[7 * rows :]
+        tails = [roll(last, -2 * g) for g in range(5)]
+        lo = 3 * rows
+        sides = close([
+            jnp.concatenate([got[: 2 * rows], mid], axis=0),
+            jnp.concatenate([got[2 * rows : 4 * rows], roll(mid, -2, 0)], axis=0),
+            jnp.concatenate([got[4 * rows : 6 * rows], roll(mid, -4, 0)], axis=0),
+            jnp.where(tail[:lo] > 0.5, jnp.concatenate(tails[:3], axis=0), 0.0),
+        ], 0)
+        extra = around(2, 0, sides)
         weights = extra[0:1]
         lap_t = wet[0:1] * (extra[1:2] - weights * t_sum)
-        lap_s = wet * (around(1) - weights * s)
+        lap_s = wet * (around(1, 0, sides) - weights * s)
         sums = running(lap_s, True)
         copies = []
         if depth > 1:
@@ -272,26 +326,18 @@
                 send(carry_s.at[r], carry_r.at[r, o], c_send.at[r, o], c_recv.at[r, o], in_depth(o))
                 for o in range(1, depth)
             ]
-        lap_m = wet * (around(0) - weights * m)
-        lap_w = wet * (around(2) - weights * w_m)
-        lap_u = wet * (around(3) - weights * u)
-        m_next = m + mdif * lap_m + press * sums
-        lm_next = lm + lap_w + 0.2 * lt
-
-        for copy in edge_copies:
-            copy.wait_recv()
-
-        def vertical(q, which):
-            above, below = q[0:1], q[rows - 1 : rows]
-            if depth > 1:
-                above = edge_r[r, 0, which : which + 1] * has_above + above * (1.0 - has_above)
-                below = edge_r[r, 1, which : which + 1] * has_below + below * (1.0 - has_below)
-            up = jnp.where(level == 0, above, roll(q, 1, 0))
-            down = jnp.where(level == rows - 1, below, roll(q, rows - 1, 0))
-            return (up - q) + (down - q)
-
-        s_next = s + tdif * lap_s + mix * vertical(s, 0) + 0.2 * m
-        lt_next = lt + lap_u + vertical(mixed, 1)
+        m_next = m + mdif * (wet * (around(0, 0, sides) - weights * m)) + press * sums
+        s_next = s_next + tdif * lap_s
+
+        got = receive(1)
+        sides = close([
+            got[: 2 * rows],
+            got[2 * rows : 4 * rows],
+            got[4 * rows :],
+            jnp.where(tail[: 2 * rows] > 0.5, jnp.concatenate(tails[3:], axis=0), 0.0),
+        ], lo)
+        lm_next = lm_next + wet * (around(3, lo, sides) - weights * w_m)
+        lt_next = lt_next + wet * (around(4, lo, sides) - weights * u)
         for o in range(1, depth):
             copies[o - 1].wait_recv()
             origin = lax.rem(d + depth - o, depth)
@@ -344,8 +390,11 @@
                 pltpu.VMEM((outer, 8, LANES), jnp.int32),
                 pltpu.SMEM((outer, 8, LANES), jnp.int32),
                 pltpu.VMEM((total, WIDTH), f32),
-                pltpu.VMEM((inner, 14, rows, LANES), f32),
-                pltpu.VMEM((inner, 14, rows, LANES), f32),
+                pltpu.VMEM((total, WIDTH), f32),
+                pltpu.VMEM((inner, 8, rows, LANES), f32),
+                pltpu.VMEM((inner, 6, rows, LANES), f32),
+                pltpu.VMEM((inner, 8, rows, LANES), f32),
+                pltpu.VMEM((inner, 6, rows, LANES), f32),
                 pltpu.VMEM((2, outer, 14, rows, LANES), f32),
                 pltpu.VMEM((2, outer, 14, rows, LANES), f32),
                 pltpu.VMEM((2, 2, 2, CELLS), f32),
@@ -353,8 +402,8 @@
                 pltpu.VMEM((2, 2, CELLS), f32),
                 pltpu.VMEM((2, depth, 2, CELLS), f32),
                 dma((11,)), dma((outer,)), dma((outer,)), dma(()),
-                dma((2, inner)), dma((2, inner)),
-                dma((2, outer)), dma((2, outer)),
+                dma((2, 2, inner)), dma((2, 2, inner)),
+                dma((2, 2, outer)), dma((2, 2, outer)),
                 dma((2, 2)), dma((2, 2)),
                 dma((2, depth)), dma((2, depth)),
             ],

time: 34.6 us -> 32.3 us (0.934)
  Pallas kernels: 33.8 us -> 31.5 us
    pallas_call x1, Pallas kernels: 31.8 us -> 29.5 us  [local(): pl.pallas_call(functools.partial(kernel, inner, outer, depth, rows * dept...]
where the time goes in v4:
time: 32.3 us; the launch traced here: 32.2 us
  Pallas kernels  31.5 us (98%)
  between operations  0.64 us (2%)
    pallas_call x1, Pallas kernels, local(): pl.pallas_call(functools.partial(kernel, inner, outer, depth, rows * dept...  29.5 us
    pallas_call x1, Pallas kernels, local(): pl.pallas_call(write_out, out_shape=(shape,) * 4, in_specs=[pl.BlockSpec(...  1.98 us

profile of v4, /device:TPU:0, one launch (start us, length us, event | category | flops | bytes accessed | tf_op | source)
XLA Modules:
  0.0 32.2 jit_solution(13606370842785429362)
XLA Ops:
  0.6 29.5 %shard_map.138 = (f32[1,8,6300]{2,1,0:T(8,128)}, f32[1,8,6300]{2,1,0:T(8,128)}, f32[1,8,6300]{2,1,0:T(8,128)}, f32[1,8,6300]{2,1,0:T(8,128)}) custom-call(f32[1,8,6300]{2,1,0:T(8,128)} %mom_hbm.1, f32[1,8,6300]{2,1,0:T(8,128)} %tra_hbm.1, f32[1,8,6300]{2,1,0:T(8,128)} %mdif_hbm.1, f32[1,8,6300]{2,1,0:T(8,128)} %tdif_hbm.1, f32[1,8,6300]{2,1,0:T(8,128)} %mix_hbm.1, ...), custom_call_target="tpu_custom_call" | custom-call | tf_op jit(solution)/shard_map/pallas_call | solution.py:382
  30.2 2.0 %shard_map.139 = (f32[1,8,6300]{2,1,0:T(8,128)}, f32[1,8,6300]{2,1,0:T(8,128)}, f32[1,8,6300]{2,1,0:T(8,128)}, f32[1,8,6300]{2,1,0:T(8,128)}) custom-call(f32[1,8,6300]{2,1,0:T(8,128)} %get-tuple-element.8.refs_0_, f32[1,8,6300]{2,1,0:T(8,128)} %get-tuple-element.9.refs_1_, f32[1,8,6300]{2,1,0:T(8,128)} %get-tuple-element.10.refs_2_, ...), custom_call_target="tpu_custom_call" | custom-call | tf_op jit(solution)/shard_map/pallas_call | solution.py:414

commit v5 on v4

--- a/solution.py
+++ b/solution.py
@@ -285,9 +285,11 @@
             count = strips[0].shape[0]
             here, own, parity = slice(lo, lo + count), lane[:count], odd[:count]
             ends = tail[:count] > 0.5
-            north = dot(strips[0], rev_i) * flip[0] + strips[0] * (1.0 - flip[0])
-            south = dot(strips[1], rev_i) * flip[1] + strips[1] * (1.0 - flip[1])
-            one, two = dot(strips[2], turn), dot(strips[3], turn)
+            turned = dot(jnp.concatenate(strips[:2], axis=0), rev_i)
+            north = turned[:count] * flip[0] + strips[0] * (1.0 - flip[0])
+            south = turned[count:] * flip[1] + strips[1] * (1.0 - flip[1])
+            turned = dot(jnp.concatenate(strips[2:], axis=0), turn)
+            one, two = turned[:count], turned[count:]
             ew_flip = jnp.where(parity, flip[2], flip[3]) > 0.5
             ew_one = jnp.where(ew_flip, jnp.where(ends, two, one), strips[2])
             ew_two = jnp.where(ew_flip, jnp.where(ends, one, 0.0), strips[3])

time: 32.3 us -> 32.2 us (level)
  no operation moved by 1% of the time
where the time goes in v5:
time: 32.2 us; the launch traced here: 32 us
  Pallas kernels  31.3 us (97%)
  between operations  0.64 us (2%)
    pallas_call x1, Pallas kernels, local(): pl.pallas_call(functools.partial(kernel, inner, outer, depth, rows * dept...  29.4 us
    pallas_call x1, Pallas kernels, local(): pl.pallas_call(write_out, out_shape=(shape,) * 4, in_specs=[pl.BlockSpec(...  1.98 us

profile of v5, /device:TPU:0, one launch (start us, length us, event | category | flops | bytes accessed | tf_op | source)
XLA Modules:
  0.0 32.0 jit_solution(2191206174304925120)
XLA Ops:
  0.6 29.4 %shard_map.138 = (f32[1,8,6300]{2,1,0:T(8,128)}, f32[1,8,6300]{2,1,0:T(8,128)}, f32[1,8,6300]{2,1,0:T(8,128)}, f32[1,8,6300]{2,1,0:T(8,128)}) custom-call(f32[1,8,6300]{2,1,0:T(8,128)} %mom_hbm.1, f32[1,8,6300]{2,1,0:T(8,128)} %tra_hbm.1, f32[1,8,6300]{2,1,0:T(8,128)} %mdif_hbm.1, f32[1,8,6300]{2,1,0:T(8,128)} %tdif_hbm.1, f32[1,8,6300]{2,1,0:T(8,128)} %mix_hbm.1, ...), custom_call_target="tpu_custom_call" | custom-call | tf_op jit(solution)/shard_map/pallas_call | solution.py:384
  30.0 2.0 %shard_map.139 = (f32[1,8,6300]{2,1,0:T(8,128)}, f32[1,8,6300]{2,1,0:T(8,128)}, f32[1,8,6300]{2,1,0:T(8,128)}, f32[1,8,6300]{2,1,0:T(8,128)}) custom-call(f32[1,8,6300]{2,1,0:T(8,128)} %get-tuple-element.8.refs_0_, f32[1,8,6300]{2,1,0:T(8,128)} %get-tuple-element.9.refs_1_, f32[1,8,6300]{2,1,0:T(8,128)} %get-tuple-element.10.refs_2_, ...), custom_call_target="tpu_custom_call" | custom-call | tf_op jit(solution)/shard_map/pallas_call | solution.py:416
